TPU v7x, 32 devices: a whole 2x2x4 slice. The times are simulated.
32 devices in a mesh: gx: 8 (over z, y), gy: 4 (over x, core).
Axes of the slice: x: 2, y: 2, z: 4, core: 2. Of those that a mesh axis runs over, the one named last changes fastest.
Arguments:
- mass_per_volume: float32 [16, 256, 512], P(None, 'gx', 'gy'), may hold values from 0.5 to 2
- momentum: float32 [3, 16, 256, 512], P(None, None, 'gx', 'gy'), may hold values from -1 to 1
- energy: float32 [16, 256, 512], P(None, 'gx', 'gy'), may hold values from 4 to 6
Outputs:
- updated_state: float32 [5, 16, 256, 512], P(None, None, 'gx', 'gy')
All inputs are finite; a program needn't handle non-finite values.
Results may differ from a plain program's by a relative error of at most 0.00012.
Values sent between devices are 32-bit elements; how exact they have to be, the bound alone decides.
A program may use at most 64 MiB of HBM per device.

v0:
```python
import functools
import jax
import jax.numpy as jnp
import numpy as np
from jax import lax
from jax.experimental import pallas as pl
from jax.experimental.pallas import tpu as pltpu
from jax.sharding import PartitionSpec as P

viscosity = 0.1
conductivity = 0.1 * 1.4 / (0.4 * 0.72)
MESH = pl.DeviceIdType.MESH
WEIGHTS = {1: 0.75, -1: -0.75, 2: -0.15, -2: 0.15, 3: 1.0 / 60.0, -3: -1.0 / 60.0}
GROUPS = ((0, 2), (2, 5))


def local_inverse(length, coefficient):
    matrix = np.eye(length)
    matrix += coefficient * (np.eye(length, k=1) - np.eye(length, k=-1))
    return np.linalg.inv(matrix)


def reduced_tables(length, count, coefficient):
    inverse = local_inverse(length, coefficient)
    alpha, beta = coefficient * inverse[:, 0], -coefficient * inverse[:, -1]
    system = np.eye(2 * count)
    for b in range(count):
        for row, at in ((2 * b, 0), (2 * b + 1, length - 1)):
            if b > 0:
                system[row, 2 * b - 1] -= alpha[at]
            if b < count - 1:
                system[row, 2 * b + 2] -= beta[at]
    g = np.linalg.inv(system)
    up = [g[2 * b + 1, 2 * b : 2 * b + 2] for b in range(count)]
    down = [g[2 * b, 2 * b : 2 * b + 2] for b in range(count)]
    rows = []
    for b in range(count):
        prev = g[2 * b - 1] if b > 0 else np.zeros(2 * count)
        nxt = g[2 * b + 2] if b < count - 1 else np.zeros(2 * count)
        t = []
        for line in (prev, nxt):
            for d in range(1, count):
                other = (b - d) % count
                basis = up[other] if other < b else down[other]
                part = line[2 * other : 2 * other + 2]
                t.append(part @ basis / (basis @ basis))
        own = [*prev[2 * b : 2 * b + 2], *nxt[2 * b : 2 * b + 2]]
        rows.append([*up[b], *down[b], *own, *t])
    return np.asarray(rows).astype(np.float32), alpha, beta


def pivots(length, coefficient):
    inverse_pivot = np.ones(length)
    for i in range(1, length):
        inverse_pivot[i] = 1.0 / (1.0 + coefficient * coefficient * inverse_pivot[i - 1])
    return inverse_pivot


def lane_tables(ly, coefficient, alpha, beta):
    inverse = local_inverse(ly, coefficient)
    dy = np.zeros((ly, ly))
    for j in range(ly):
        for k, w in WEIGHTS.items():
            if 0 <= j + k < ly:
                dy[j + k, j] = w
    sel = np.zeros((5, 32, ly))
    ed = np.zeros((5, 32, ly))
    wy = np.zeros((5, 16, ly))
    ey = np.zeros((5, 16, ly))
    for f in range(5):
        for k in range(3):
            sel[f, 3 * f + k, k] = 1.0
            sel[f, 16 + 3 * f + k, ly - 3 + k] = 1.0
            for row, position in ((3 * f + k, k - 3), (16 + 3 * f + k, ly + k)):
                for step, w in WEIGHTS.items():
                    if 0 <= position - step < ly:
                        ed[f, row, position - step] = w
        wy[f, f], wy[f, 8 + f] = inverse[0], inverse[-1]
        ey[f, f], ey[f, 8 + f] = alpha, beta
    parts = [dy, inverse.T, sel.reshape(-1, ly), ed.reshape(-1, ly), wy.reshape(-1, ly), ey.reshape(-1, ly)]
    return np.concatenate(parts, 0).astype(np.float32)


def dot(a, b, dims):
    return lax.dot_general(
        a, b, (dims, ((), ())), precision=lax.Precision.HIGHEST, preferred_element_type=jnp.float32
    )


NN, NT, TN = ((1,), (0,)), ((1,), (1,)), ((0,), (0,))


def difference(at):
    return 0.75 * (at(1) - at(-1)) - 0.15 * (at(2) - at(-2)) + (1.0 / 60.0) * (at(3) - at(-3))


def around(v):
    n = v.shape[0]
    return difference(lambda k: pltpu.roll(v, (-k) % n, 0))


def kernel(
    nx, ny, lx, lz, ly, coefficient, ipiv, alpha, beta,
    mass, mom, energy, tab, xt, yt, out,
    xp, pt, ept, mt, gy, fxp, fy, dz, inc, ysend, yhalo, ysend2, yhalo2,
    xs, xr, ws, wr,
    hss, hrs, xss, xrs, wss, wrs,
):
    ix, iy = lax.axis_index("gx"), lax.axis_index("gy")
    rows = lx * lz

    barrier = pltpu.get_barrier_semaphore()
    for d in range(1, nx):
        pl.semaphore_signal(barrier, inc=1, device_id={"gx": lax.rem(ix + d, nx)}, device_id_type=MESH)
    for d in range(1, ny):
        pl.semaphore_signal(barrier, inc=1, device_id={"gy": lax.rem(iy + d, ny)}, device_id_type=MESH)

    o = 2 * ly
    dy = tab.at[pl.ds(0, ly)]
    inverse = tab.at[pl.ds(ly, ly)]

    def sel(f):
        return tab[o + 32 * f : o + 32 * f + 32]

    def ed(f):
        return tab[o + 160 + 32 * f : o + 160 + 32 * f + 32]

    def wy(f):
        return tab[o + 320 + 16 * f : o + 320 + 16 * f + 16]

    def ey(f):
        return tab[o + 400 + 16 * f : o + 400 + 16 * f + 16]

    def flat(v):
        return v.reshape(rows, ly)

    def primitives(i, _=None):
        at = pl.ds(i, lz, stride=lx)
        rho, e = mass[at, :], energy[at, :]
        m = [mom[k, at, :] for k in range(3)]
        inv = 1.0 / rho
        u = [a * inv for a in m]
        p = 0.4 * (e - 0.5 * (m[0] * u[0] + m[1] * u[1] + m[2] * u[2]))
        for k in range(3):
            xp[k, i + 3] = u[k]
            mt[k, i] = m[k]
        xp[3, i + 3] = p * inv
        pt[i] = p
        ept[i] = e + p
        return 0

    edges = sorted({*range(3), *range(lx - 3, lx)})
    for i in edges:
        primitives(i)

    zeros3 = jnp.zeros((3, lz, ly), jnp.float32)

    def x_halo(ref, fields, base):
        to_next = pltpu.make_async_remote_copy(
            ref.at[:, pl.ds(lx, 3)], ref.at[:, pl.ds(0, 3)], hss.at[base], hrs.at[base],
            device_id={"gx": ix + 1}, device_id_type=MESH)
        to_prev = pltpu.make_async_remote_copy(
            ref.at[:, pl.ds(3, 3)], ref.at[:, pl.ds(lx + 3, 3)], hss.at[base + 1], hrs.at[base + 1],
            device_id={"gx": ix - 1}, device_id_type=MESH)

        @pl.when(ix == 0)
        def _():
            for f in range(fields):
                ref[f, 0:3] = zeros3

        @pl.when(ix == nx - 1)
        def _():
            for f in range(fields):
                ref[f, lx + 3 : lx + 6] = zeros3

        return to_next, to_prev, ix, nx

    def y_halo(source, ref, base):
        to_next = pltpu.make_async_remote_copy(
            source.at[pl.ds(16, 16)], ref.at[pl.ds(0, 16)], hss.at[base], hrs.at[base],
            device_id={"gy": iy + 1}, device_id_type=MESH)
        to_prev = pltpu.make_async_remote_copy(
            source.at[pl.ds(0, 16)], ref.at[pl.ds(16, 16)], hss.at[base + 1], hrs.at[base + 1],
            device_id={"gy": iy - 1}, device_id_type=MESH)

        @pl.when(iy == 0)
        def _():
            ref[0:16] = jnp.zeros((16, rows), jnp.float32)

        @pl.when(iy == ny - 1)
        def _():
            ref[16:32] = jnp.zeros((16, rows), jnp.float32)

        return to_next, to_prev, iy, ny

    def start(halo):
        to_next, to_prev, here, count = halo
        pl.when(here < count - 1)(to_next.start)
        pl.when(here > 0)(to_prev.start)

    def arrive(halo):
        to_next, to_prev, here, count = halo
        pl.when(here > 0)(to_next.wait_recv)
        pl.when(here < count - 1)(to_prev.wait_recv)

    def sent(halo):
        to_next, to_prev, here, count = halo
        pl.when(here < count - 1)(to_next.wait_send)
        pl.when(here > 0)(to_prev.wait_send)

    h1x = x_halo(xp, 4, 0)
    pl.semaphore_wait(barrier, nx + ny - 2)
    start(h1x)
    lax.fori_loop(3, lx - 3, primitives, 0, unroll=2)

    packed = dot(sel(0), flat(xp[0, 3 : lx + 3]), NT)
    for f in range(1, 4):
        packed += dot(sel(f), flat(xp[f, 3 : lx + 3]), NT)
    ysend[...] = packed
    h1y = y_halo(ysend, yhalo, 2)
    start(h1y)
    for f in range(4):
        gy[f] = dot(flat(xp[f, 3 : lx + 3]), dy[...], NN).reshape(lx, lz, ly)
    arrive(h1y)
    for f in range(4):
        gy[f] += dot(yhalo[...], ed(f), TN).reshape(lx, lz, ly)
    arrive(h1x)

    def fluxes(i, _=None):
        u = [xp[k, i + 3] for k in range(3)]
        m = [mt[k, i] for k in range(3)]
        p, ep = pt[i], ept[i]
        g = [
            [difference(lambda k: xp[f, i + 3 + k]) for f in range(4)],
            [gy[f, i] for f in range(4)],
            [around(xp[f, i + 3]) for f in range(4)],
        ]
        dilation = (2.0 / 3.0 * viscosity) * (g[0][0] + g[1][1] + g[2][2])
        stress = {}
        for a in range(3):
            for b in range(a, 3):
                s = viscosity * (g[a][b] + g[b][a])
                if a == b:
                    s = s - dilation
                stress[a, b] = stress[b, a] = s
        for j in range(3):
            entries = [m[j]]
            for k in range(3):
                e = m[k] * u[j] - stress[k, j]
                entries.append(e + p if k == j else e)
            power = u[0] * stress[0, j] + u[1] * stress[1, j] + u[2] * stress[2, j]
            entries.append(ep * u[j] - power - conductivity * g[j][3])
            for c in range(5):
                if j == 0:
                    fxp[c, i + 3] = entries[c]
                elif j == 1:
                    fy[c, i] = entries[c]
                else:
                    dz[c, i] = around(entries[c])
        return 0

    for i in edges:
        fluxes(i)
    h2x = x_halo(fxp, 5, 4)
    start(h2x)
    lax.fori_loop(3, lx - 3, fluxes, 0)

    packed = dot(sel(0), flat(fy[0]), NT)
    for f in range(1, 5):
        packed += dot(sel(f), flat(fy[f]), NT)
    ysend2[...] = packed
    h2y = y_halo(ysend2, yhalo2, 6)
    start(h2y)
    for c in range(5):
        dz[c] += dot(flat(fy[c]), dy[...], NN).reshape(lx, lz, ly)
    arrive(h2y)
    for c in range(5):
        dz[c] += dot(yhalo2[...], ed(c), TN).reshape(lx, lz, ly)
    arrive(h2x)

    width = 8 + 2 * (nx - 1)

    def xtab(k):
        return xt[ix * width + k]

    copies = []
    ends = {}
    for g, (f0, f1) in enumerate(GROUPS):
        v = [None] * 5
        for i in range(lx):
            for f in range(f0, f1):
                s = difference(lambda k: fxp[f, i + 3 + k]) + dz[f, i]
                s = s * (-2.0 * coefficient)
                v[f] = s if i == 0 else (s + coefficient * v[f]) * float(ipiv[i])
                inc[f, i] = v[f]
        last = list(v)
        for i in range(lx - 2, -1, -1):
            for f in range(f0, f1):
                v[f] = inc[f, i] - float(coefficient * ipiv[i]) * v[f]
                inc[f, i] = v[f]
        for f in range(f0, f1):
            ends[f] = (v[f], last[f])
            xs[0, f] = xtab(0) * v[f] + xtab(1) * last[f]
            xs[1, f] = xtab(2) * v[f] + xtab(3) * last[f]
        for d in range(1, nx):
            which = jnp.where(ix + d >= nx, 1, 0).astype(jnp.int32)
            copy = pltpu.make_async_remote_copy(
                xs.at[which, pl.ds(f0, f1 - f0)], xr.at[d - 1, pl.ds(f0, f1 - f0)],
                xss.at[g, d - 1], xrs.at[g, d - 1],
                device_id={"gx": lax.rem(ix + d, nx)}, device_id_type=MESH)
            copy.start()
            copies.append((g, d, copy))

    edges_y = None
    for g, (f0, f1) in enumerate(GROUPS):
        for group, d, copy in copies:
            if group == g:
                copy.wait_recv()
        for f in range(f0, f1):
            y0, yl = inc[f, 0], inc[f, lx - 1]
            before = xtab(4) * y0 + xtab(5) * yl
            after = xtab(6) * y0 + xtab(7) * yl
            for d in range(1, nx):
                r = xr[d - 1, f]
                before += xtab(7 + d) * r
                after += xtab(7 + nx - 1 + d) * r
            for i in range(lx):
                inc[f, i] += float(alpha[i]) * before + float(beta[i]) * after
            part = dot(wy(f), flat(inc[f]), NT)
            edges_y = part if edges_y is None else edges_y + part

    ywidth = 8 + 2 * (ny - 1)

    def ytab(k):
        return yt[iy * ywidth + k]

    y0, yl = edges_y[0:8], edges_y[8:16]
    ws[0] = ytab(0) * y0 + ytab(1) * yl
    ws[1] = ytab(2) * y0 + ytab(3) * yl
    ycopies = []
    for d in range(1, ny):
        which = jnp.where(iy + d >= ny, 1, 0).astype(jnp.int32)
        copy = pltpu.make_async_remote_copy(
            ws.at[which], wr.at[d - 1], wss.at[d - 1], wrs.at[d - 1],
            device_id={"gy": lax.rem(iy + d, ny)}, device_id_type=MESH)
        copy.start()
        ycopies.append(copy)
    for f in range(5):
        gy5 = dot(flat(inc[f]), inverse[...], NN)
        inc[f] = gy5.reshape(lx, lz, ly)
    before = ytab(4) * y0 + ytab(5) * yl
    after = ytab(6) * y0 + ytab(7) * yl
    for d in range(1, ny):
        ycopies[d - 1].wait_recv()
        r = wr[d - 1]
        before += ytab(7 + d) * r
        after += ytab(7 + ny - 1 + d) * r
    outside = jnp.concatenate([before, after], 0)
    for f in range(5):
        total = (flat(inc[f]) + dot(outside, ey(f), TN)).reshape(lx, lz, ly)
        for i in range(lx):
            at = pl.ds(i, lz, stride=lx)
            state = mass[at, :] if f == 0 else (energy[at, :] if f == 4 else mt[f - 1, i])
            out[f, at, :] = state + total[i]

    for halo in (h1x, h1y, h2x, h2y):
        sent(halo)
    for _, _, copy in copies:
        copy.wait_send()
    for copy in ycopies:
        copy.wait_send()


def body(nx, ny, mass, mom, energy):
    lz, lx, ly = mass.shape
    rows = lx * lz
    coefficient = float(max(lx, ly))
    xtab, xa, xb = reduced_tables(lx, nx, coefficient)
    ytab, ya, yb = reduced_tables(ly, ny, coefficient)
    tab = lane_tables(ly, coefficient, ya, yb)
    vm = pl.BlockSpec(memory_space=pltpu.VMEM)
    sm = pl.BlockSpec(memory_space=pltpu.SMEM)
    f32 = jnp.float32
    groups = len(GROUPS)
    block = (lx, lz, ly)
    dma = pltpu.SemaphoreType.DMA
    result = pl.pallas_call(
        functools.partial(kernel, nx, ny, lx, lz, ly, coefficient, pivots(lx, coefficient), xa, xb),
        out_shape=jax.ShapeDtypeStruct((5, rows, ly), f32),
        in_specs=[vm, vm, vm, vm, sm, sm],
        out_specs=vm,
        scratch_shapes=[
            pltpu.VMEM((4, lx + 6, lz, ly), f32),
            pltpu.VMEM(block, f32),
            pltpu.VMEM(block, f32),
            pltpu.VMEM((3, *block), f32),
            pltpu.VMEM((4, *block), f32),
            pltpu.VMEM((5, lx + 6, lz, ly), f32),
            pltpu.VMEM((5, *block), f32),
            pltpu.VMEM((5, *block), f32),
            pltpu.VMEM((5, *block), f32),
            pltpu.VMEM((32, rows), f32),
            pltpu.VMEM((32, rows), f32),
            pltpu.VMEM((32, rows), f32),
            pltpu.VMEM((32, rows), f32),
            pltpu.VMEM((2, 5, lz, ly), f32),
            pltpu.VMEM((nx - 1, 5, lz, ly), f32),
            pltpu.VMEM((2, 8, rows), f32),
            pltpu.VMEM((ny - 1, 8, rows), f32),
            dma((8,)),
            dma((8,)),
            dma((groups, nx - 1)),
            dma((groups, nx - 1)),
            dma((ny - 1,)),
            dma((ny - 1,)),
        ],
        compiler_params=pltpu.CompilerParams(
            collective_id=0, has_side_effects=True, vmem_limit_bytes=48 * 2**20
        ),
    )(
        mass.reshape(rows, ly), mom.reshape(3, rows, ly), energy.reshape(rows, ly),
        jnp.asarray(tab), jnp.asarray(xtab.reshape(-1)), jnp.asarray(ytab.reshape(-1)),
    )
    return result.reshape(5, lz, lx, ly)


def solution(mesh):
    return jax.shard_map(
        functools.partial(body, mesh.shape["gx"], mesh.shape["gy"]),
        mesh=mesh,
        in_specs=(P(None, "gx", "gy"), P(None, None, "gx", "gy"), P(None, "gx", "gy")),
        out_specs=P(None, None, "gx", "gy"),
        check_vma=False,
    )
```

profile of v0, /device:TPU:1, one launch (start us, length us, event | category | flops | bytes accessed | tf_op | source)
XLA Modules:
  0.0 40.8 jit_solution(13178802647392937900)
XLA Ops:
  0.0 0.0 copy-start
  0.0 1.1 %copy-done = f32[3,16,32,128]{3,2,1,0:T(8,128)S(1)} copy-done((f32[3,16,32,128]{3,2,1,0:T(8,128)S(1)}, f32[3,16,32,128]{3,2,1,0:T(8,128)}, u32[]{:S(2)}) %copy-start) | copy-done | bytes 786456
  1.1 0.0 copy-start.1
  1.1 1.0 %copy-done.1 = f32[736,128]{1,0:T(8,128)S(1)} copy-done((f32[736,128]{1,0:T(8,128)S(1)}, f32[736,128]{1,0:T(8,128)}, u32[]{:S(2)}) %copy-start.1) | copy-done | bytes 376856
  2.1 0.0 copy-start.2
  2.1 0.9 %copy-done.2 = f32[16,32,128]{2,1,0:T(8,128)S(1)} copy-done((f32[16,32,128]{2,1,0:T(8,128)S(1)}, f32[16,32,128]{2,1,0:T(8,128)}, u32[]{:S(2)}) %copy-start.2) | copy-done | bytes 262168
  3.1 0.0 copy-start.3
  3.1 0.9 %copy-done.3 = f32[16,32,128]{2,1,0:T(8,128)S(1)} copy-done((f32[16,32,128]{2,1,0:T(8,128)S(1)}, f32[16,32,128]{2,1,0:T(8,128)}, u32[]{:S(2)}) %copy-start.3) | copy-done | bytes 262168
  4.0 0.0 copy-start.4
  4.0 0.7 %copy-done.4 = f32[176]{0:T(256)S(1)} copy-done((f32[176]{0:T(256)S(1)}, f32[176]{0:T(256)}, u32[]{:S(2)}) %copy-start.4) | copy-done | bytes 728
  4.7 0.0 copy-start.5
  4.7 0.7 %copy-done.5 = f32[56]{0:T(128)S(1)} copy-done((f32[56]{0:T(128)S(1)}, f32[56]{0:T(128)}, u32[]{:S(2)}) %copy-start.5) | copy-done | bytes 248
  5.4 34.4 %shard_map.64 = f32[5,512,128]{2,1,0:T(8,128)S(1)} custom-call(f32[512,128]{1,0:T(8,128)S(1)} %bitcast.6, f32[3,512,128]{2,1,0:T(8,128)S(1)} %bitcast.5, f32[512,128]{1,0:T(8,128)S(1)} %bitcast.7, f32[736,128]{1,0:T(8,128)S(1)} %copy-done.1, f32[176]{0:T(256)S(1)} %copy-done.4, f32[56]{0:T(128)S(1)} %copy-done.5), custom_call_target="tpu_custom_call" | custom-call | tf_op jit(solution)/shard_map/pallas_call | solution.py:387
  39.7 1.1 %copy.8 = f32[5,16,32,128]{3,2,1,0:T(8,128)} copy(f32[5,16,32,128]{3,2,1,0:T(8,128)S(1)} %bitcast.4) | data formatting | bytes 2621440
Async XLA Ops:
  0.0 1.1 %copy-start = (f32[3,16,32,128]{3,2,1,0:T(8,128)S(1)}, f32[3,16,32,128]{3,2,1,0:T(8,128)}, u32[]{:S(2)}) copy-start(f32[3,16,32,128]{3,2,1,0:T(8,128)} %param.7) | copy-start | bytes 2359300
  1.1 1.0 %copy-start.1 = (f32[736,128]{1,0:T(8,128)S(1)}, f32[736,128]{1,0:T(8,128)}, u32[]{:S(2)}) copy-start(f32[736,128]{1,0:T(8,128)} %constant.6.clone.tab) | copy-start | bytes 1130500
  2.1 0.9 %copy-start.2 = (f32[16,32,128]{2,1,0:T(8,128)S(1)}, f32[16,32,128]{2,1,0:T(8,128)}, u32[]{:S(2)}) copy-start(f32[16,32,128]{2,1,0:T(8,128)} %param.6) | copy-start | bytes 786436
  3.1 0.9 %copy-start.3 = (f32[16,32,128]{2,1,0:T(8,128)S(1)}, f32[16,32,128]{2,1,0:T(8,128)}, u32[]{:S(2)}) copy-start(f32[16,32,128]{2,1,0:T(8,128)} %param.8) | copy-start | bytes 786436
  4.0 0.7 %copy-start.4 = (f32[176]{0:T(256)S(1)}, f32[176]{0:T(256)}, u32[]{:S(2)}) copy-start(f32[176]{0:T(256)} %constant.7.clone.xt) | copy-start | bytes 2116
  4.7 0.7 %copy-start.5 = (f32[56]{0:T(128)S(1)}, f32[56]{0:T(128)}, u32[]{:S(2)}) copy-start(f32[56]{0:T(128)} %constant.8.clone.yt) | copy-start | bytes 676
where the time goes:
time: 41.5 us; the launch traced here: 40.8 us
  Pallas kernels  34.4 us (83%)
  local copies, waits for them, and re-layouts  6.41 us (15%)
    pallas_call x1, Pallas kernels, body(): pl.pallas_call(functools.partial(kernel, nx, ny, lx, lz, ly, coefficient,...  34.4 us
    unnamed x13, local copies, waits for them, and re-layouts  6.41 us

commit v1 on v0

--- a/solution.py
+++ b/solution.py
@@ -101,10 +101,11 @@
 
 def kernel(
     nx, ny, lx, lz, ly, coefficient, ipiv, alpha, beta,
-    mass, mom, energy, tab, xt, yt, out,
+    mass_in, mom_in, energy_in, tab_in, xt_in, yt_in, out,
+    mass, mom, energy, tab, xt, yt,
     xp, pt, ept, mt, gy, fxp, fy, dz, inc, ysend, yhalo, ysend2, yhalo2,
     xs, xr, ws, wr,
-    hss, hrs, xss, xrs, wss, wrs,
+    hss, hrs, xss, xrs, wss, wrs, lsem,
 ):
     ix, iy = lax.axis_index("gx"), lax.axis_index("gy")
     rows = lx * lz
@@ -114,6 +115,14 @@
         pl.semaphore_signal(barrier, inc=1, device_id={"gx": lax.rem(ix + d, nx)}, device_id_type=MESH)
     for d in range(1, ny):
         pl.semaphore_signal(barrier, inc=1, device_id={"gy": lax.rem(iy + d, ny)}, device_id_type=MESH)
+
+    loads = [
+        pltpu.make_async_copy(a, b, lsem.at[k])
+        for k, (a, b) in enumerate((
+            (mass_in, mass), (mom_in, mom), (energy_in, energy), (tab_in, tab), (xt_in, xt), (yt_in, yt)))
+    ]
+    for load in loads:
+        load.start()
 
     o = 2 * ly
     dy = tab.at[pl.ds(0, ly)]
@@ -149,6 +158,8 @@
         ept[i] = e + p
         return 0
 
+    for load in loads[:3]:
+        load.wait()
     edges = sorted({*range(3), *range(lx - 3, lx)})
     for i in edges:
         primitives(i)
@@ -209,15 +220,17 @@
         pl.when(here > 0)(to_prev.wait_send)
 
     h1x = x_halo(xp, 4, 0)
-    pl.semaphore_wait(barrier, nx + ny - 2)
-    start(h1x)
     lax.fori_loop(3, lx - 3, primitives, 0, unroll=2)
+    for load in loads[3:]:
+        load.wait()
 
     packed = dot(sel(0), flat(xp[0, 3 : lx + 3]), NT)
     for f in range(1, 4):
         packed += dot(sel(f), flat(xp[f, 3 : lx + 3]), NT)
     ysend[...] = packed
     h1y = y_halo(ysend, yhalo, 2)
+    pl.semaphore_wait(barrier, nx + ny - 2)
+    start(h1x)
     start(h1y)
     for f in range(4):
         gy[f] = dot(flat(xp[f, 3 : lx + 3]), dy[...], NN).reshape(lx, lz, ly)
@@ -379,7 +392,7 @@
     ytab, ya, yb = reduced_tables(ly, ny, coefficient)
     tab = lane_tables(ly, coefficient, ya, yb)
     vm = pl.BlockSpec(memory_space=pltpu.VMEM)
-    sm = pl.BlockSpec(memory_space=pltpu.SMEM)
+    hbm = pl.BlockSpec(memory_space=pltpu.HBM)
     f32 = jnp.float32
     groups = len(GROUPS)
     block = (lx, lz, ly)
@@ -387,9 +400,15 @@
     result = pl.pallas_call(
         functools.partial(kernel, nx, ny, lx, lz, ly, coefficient, pivots(lx, coefficient), xa, xb),
         out_shape=jax.ShapeDtypeStruct((5, rows, ly), f32),
-        in_specs=[vm, vm, vm, vm, sm, sm],
+        in_specs=[hbm] * 6,
         out_specs=vm,
         scratch_shapes=[
+            pltpu.VMEM((rows, ly), f32),
+            pltpu.VMEM((3, rows, ly), f32),
+            pltpu.VMEM((rows, ly), f32),
+            pltpu.VMEM(tab.shape, f32),
+            pltpu.SMEM((xtab.size,), f32),
+            pltpu.SMEM((ytab.size,), f32),
             pltpu.VMEM((4, lx + 6, lz, ly), f32),
             pltpu.VMEM(block, f32),
             pltpu.VMEM(block, f32),
@@ -413,14 +432,15 @@
             dma((groups, nx - 1)),
             dma((ny - 1,)),
             dma((ny - 1,)),
+            dma((6,)),
         ],
         compiler_params=pltpu.CompilerParams(
-            collective_id=0, has_side_effects=True, vmem_limit_bytes=48 * 2**20
+            collective_id=0, has_side_effects=True, vmem_limit_bytes=40 * 2**20
         ),
-    )(
+    )(*[pltpu.with_memory_space_constraint(a, pltpu.HBM) for a in (
         mass.reshape(rows, ly), mom.reshape(3, rows, ly), energy.reshape(rows, ly),
         jnp.asarray(tab), jnp.asarray(xtab.reshape(-1)), jnp.asarray(ytab.reshape(-1)),
-    )
+    )])
     return result.reshape(5, lz, lx, ly)
 
 

time: 41.5 us -> 37.4 us (0.901)
  local copies, waits for them, and re-layouts: 6.41 us -> 1.06 us
  Pallas kernels: 34.4 us -> 35.8 us
    unnamed x13 -> x1, local copies, waits for them, and re-layouts: 6.41 us -> 1.06 us
    pallas_call x1, Pallas kernels: 34.4 us -> 35.8 us  [body(): pl.pallas_call(functools.partial(kernel, nx, ny, lx, lz, ly, coefficient,...]
where the time goes in v1:
time: 37.4 us; the launch traced here: 36.8 us
  Pallas kernels  35.8 us (96%)
  local copies, waits for them, and re-layouts  1.06 us (3%)
    pallas_call x1, Pallas kernels, body(): pl.pallas_call(functools.partial(kernel, nx, ny, lx, lz, ly, coefficient,...  35.8 us
    unnamed x1, local copies, waits for them, and re-layouts  1.06 us

profile of v1, /device:TPU:1, one launch (start us, length us, event | category | flops | bytes accessed | tf_op | source)
XLA Modules:
  0.0 36.8 jit_solution(14698546255070214019)
XLA Ops:
  0.0 35.8 %shard_map.64 = f32[5,512,128]{2,1,0:T(8,128)S(1)} custom-call(f32[512,128]{1,0:T(8,128)} %bitcast.6, f32[3,512,128]{2,1,0:T(8,128)} %bitcast.5, f32[512,128]{1,0:T(8,128)} %bitcast.7, f32[736,128]{1,0:T(8,128)} %constant.6.clone.tab_in, f32[176]{0:T(256)} %constant.7.clone.xt_in, f32[56]{0:T(128)} %constant.8.clone.yt_in), custom_call_target="tpu_custom_call" | custom-call | tf_op jit(solution)/shard_map/pallas_call | solution.py:400
  35.8 1.1 %copy.8 = f32[5,16,32,128]{3,2,1,0:T(8,128)} copy(f32[5,16,32,128]{3,2,1,0:T(8,128)S(1)} %bitcast.4) | data formatting | bytes 2621440

commit v2 on v1

v2 whole, which is shorter than its diff:
```python
import functools
import jax
import jax.numpy as jnp
import ml_dtypes
import numpy as np
from jax import lax
from jax.experimental import pallas as pl
from jax.experimental.pallas import tpu as pltpu
from jax.sharding import PartitionSpec as P

viscosity = 0.1
conductivity = 0.1 * 1.4 / (0.4 * 0.72)
MESH = pl.DeviceIdType.MESH
WEIGHTS = {1: 45.0, -1: -45.0, 2: -9.0, -2: 9.0, 3: 1.0, -3: -1.0}
STEP = 1.0 / 60.0


def local_inverse(length, coefficient):
    matrix = np.eye(length)
    matrix += coefficient * (np.eye(length, k=1) - np.eye(length, k=-1))
    return np.linalg.inv(matrix)


def reduced_system(length, count, coefficient):
    inverse = local_inverse(length, coefficient)
    alpha, beta = coefficient * inverse[:, 0], -coefficient * inverse[:, -1]
    system = np.eye(2 * count)
    for b in range(count):
        for row, at in ((2 * b, 0), (2 * b + 1, length - 1)):
            if b > 0:
                system[row, 2 * b - 1] -= alpha[at]
            if b < count - 1:
                system[row, 2 * b + 2] -= beta[at]
    g = np.linalg.inv(system)
    up = [g[2 * b + 1, 2 * b : 2 * b + 2] for b in range(count)]
    down = [g[2 * b, 2 * b : 2 * b + 2] for b in range(count)]
    return inverse, alpha, beta, g, up, down


def outside_lines(g, b, count):
    prev = g[2 * b - 1] if b > 0 else np.zeros(2 * count)
    nxt = g[2 * b + 2] if b < count - 1 else np.zeros(2 * count)
    return prev, nxt


def received(line, b, count, up, down):
    weights = []
    for d in range(1, count):
        other = (b - d) % count
        basis = up[other] if other < b else down[other]
        weights.append(line[2 * other : 2 * other + 2] @ basis / (basis @ basis))
    return weights


def reduced_tables(length, count, coefficient):
    inverse, alpha, beta, g, up, down = reduced_system(length, count, coefficient)
    rows = []
    for b in range(count):
        prev, nxt = outside_lines(g, b, count)
        own = [*prev[2 * b : 2 * b + 2], *nxt[2 * b : 2 * b + 2]]
        rows.append([*up[b], *down[b], *own, *received(prev, b, count, up, down), *received(nxt, b, count, up, down)])
    return np.asarray(rows).astype(np.float32), alpha, beta


def coupled_tables(length, count, coefficient, scale):
    inverse, alpha, beta, g, up, down = reduced_system(length, count, coefficient)
    ends = [0, length - 1]
    to_next, to_prev = [], []
    for m in range(3):
        n, p = np.zeros(2), np.zeros(2)
        for r in range(3 - m):
            n += scale * inverse[ends, r] * WEIGHTS[-(r + 1 + m)]
            p += scale * inverse[ends, length - 1 - r] * WEIGHTS[r + 1 + m]
        to_next.append(n)
        to_prev.append(p)
    rows = []
    for b in range(count):
        prev, nxt = outside_lines(g, b, count)

        def via(line, j, spread):
            if not 0 <= j < count:
                return [0.0] * 3
            return [line[2 * j : 2 * j + 2] @ s for s in spread]

        def ratio(line, j, basis):
            return line[2 * j : 2 * j + 2] @ basis[j] / (basis[j] @ basis[j])

        def sent(basis, t, line_at):
            if not 0 <= t < count:
                low, high = 0.0, 0.0
                ref = None
            else:
                ref = g[line_at(t)]
            out = []
            for j, spread in ((b - 1, to_prev), (b + 1, to_next)):
                if not 0 <= j < count:
                    out += [0.0] * 3
                    continue
                line = ref
                if line is None:
                    line = g[line_at(b + 1 if basis is up else b - 1)] if 0 <= (b + 1 if basis is up else b - 1) < count else None
                beyond = (j > b) if basis is up else (j < b)
                if line is None or (ref is None and beyond):
                    out += [0.0] * 3
                    continue
                scale_j = ratio(line, j, basis) / ratio(line, b, basis)
                out += [scale_j * (basis[j] @ s) for s in spread]
            return out

        u = sent(up, b + 2, lambda t: 2 * t - 1)
        d = sent(down, b - 2, lambda t: 2 * t + 2)
        own = []
        for line in (prev, nxt):
            own += [*line[2 * b : 2 * b + 2], *via(line, b - 1, to_prev), *via(line, b + 1, to_next)]
        rows.append([*up[b], *u, *down[b], *d, *own, *received(prev, b, count, up, down), *received(nxt, b, count, up, down)])
    return np.asarray(rows).astype(np.float32), inverse, alpha, beta


def pivots(length, coefficient):
    inverse_pivot = np.ones(length)
    for i in range(1, length):
        inverse_pivot[i] = 1.0 / (1.0 + coefficient * coefficient * inverse_pivot[i - 1])
    return inverse_pivot


def halves(matrix):
    high = matrix.astype(ml_dtypes.bfloat16)
    low = (matrix - high.astype(np.float64)).astype(ml_dtypes.bfloat16)
    return high.astype(np.float64), low.astype(np.float64)


def lane_tables(lx, lz, ly, coefficient, xa, xb, ya, yb):
    inverse = local_inverse(ly, coefficient)
    dy = np.zeros((ly, ly))
    for j in range(ly):
        for k, w in WEIGHTS.items():
            if 0 <= j + k < ly:
                dy[j + k, j] = w
    sel = np.zeros((5, 32, ly))
    ed = np.zeros((5, 32, ly))
    wy = np.zeros((5, 16, ly))
    ey = np.zeros((5, 16, ly))
    for f in range(5):
        for k in range(3):
            sel[f, 3 * f + k, k] = 1.0
            sel[f, 16 + 3 * f + k, ly - 3 + k] = 1.0
            for row, position in ((3 * f + k, k - 3), (16 + 3 * f + k, ly + k)):
                for step, w in WEIGHTS.items():
                    if 0 <= position - step < ly:
                        ed[f, row, position - step] = w
        wy[f, f], wy[f, 8 + f] = inverse[0], inverse[-1]
        ey[f, f], ey[f, 8 + f] = ya, yb
    spread = np.zeros((2, lz, lx, lz))
    for z in range(lz):
        spread[0, z, :, z], spread[1, z, :, z] = xa, xb
    spread = spread.reshape(2 * lz, lx * lz)
    parts = {"dy": np.concatenate([dy, dy])}
    high, low = halves(inverse.T)
    parts["inverse"] = np.concatenate([high, high, low])
    for f in range(5):
        parts["sel", f] = sel[f]
        parts["ed", f] = np.concatenate([ed[f], ed[f]])
        high, low = halves(wy[f])
        parts["wy", f] = np.concatenate([high, low])
        high, low = halves(ey[f])
        parts["ey", f] = np.concatenate([high, high, low])
    high, low = halves(spread)
    spread = np.concatenate([high, high, low])
    for c in range(lx * lz // ly):
        parts["spread", c] = spread[:, c * ly : c * ly + ly]
    places, at = {}, 0
    for name, part in parts.items():
        places[name] = (at, at + part.shape[0])
        at += part.shape[0]
    return np.concatenate(list(parts.values()), 0).astype(ml_dtypes.bfloat16), places


NN, NT, TN = ((1,), (0,)), ((1,), (1,)), ((0,), (0,))


def dot(a, b, dims):
    return lax.dot_general(a, b, (dims, ((), ())), preferred_element_type=jnp.float32)


def split(v):
    high = v.astype(jnp.bfloat16)
    low = (v - high.astype(jnp.float32)).astype(jnp.bfloat16)
    return high, low


def two(v, axis):
    return jnp.concatenate(split(v), axis)


def three(v, axis):
    high, low = split(v)
    return jnp.concatenate([high, low, high], axis)


def difference(at):
    total = None
    for k, w in ((1, 45.0), (2, -9.0), (3, 1.0)):
        a, b = at(k), at(-k)
        if a is None and b is None:
            continue
        pair = -b if a is None else (a if b is None else a - b)
        pair = pair if w == 1.0 else w * pair
        total = pair if total is None else total + pair
    return total


def around(v):
    n = v.shape[0]
    return difference(lambda k: pltpu.roll(v, (-k) % n, 0))


def kernel(
    nx, ny, lx, lz, ly, coefficient, ipiv, xinv, alpha, beta, places,
    mass_in, mom_in, energy_in, tab_in, xt_in, yt_in, out,
    mass, mom, energy, tab, xt, yt,
    xp, pt, ept, mt, gy, fxp, fy, dz, inc, ysend, yhalo, ysend2, yhalo2,
    xs, xr, ws, wr,
    hss, hrs, xss, xrs, wss, wrs, lsem,
):
    ix, iy = lax.axis_index("gx"), lax.axis_index("gy")
    rows = lx * lz
    scale = -2.0 * coefficient * STEP

    barrier = pltpu.get_barrier_semaphore()
    for d in range(1, nx):
        pl.semaphore_signal(barrier, inc=1, device_id={"gx": lax.rem(ix + d, nx)}, device_id_type=MESH)
    for d in range(1, ny):
        pl.semaphore_signal(barrier, inc=1, device_id={"gy": lax.rem(iy + d, ny)}, device_id_type=MESH)

    loads = [
        pltpu.make_async_copy(a, b, lsem.at[k])
        for k, (a, b) in enumerate((
            (mass_in, mass), (mom_in, mom), (energy_in, energy), (tab_in, tab), (xt_in, xt), (yt_in, yt)))
    ]
    for load in loads:
        load.start()

    def part(*name):
        low, high = places[name if len(name) > 1 else name[0]]
        return tab[low:high]

    def flat(v):
        return v.reshape(rows, ly)

    def block(v):
        return v.reshape(lx, lz, ly)

    def primitives(i, _=None):
        at = pl.ds(i, lz, stride=lx)
        rho, e = mass[at, :], energy[at, :]
        m = [mom[k, at, :] for k in range(3)]
        inv = 1.0 / rho
        u = [a * inv for a in m]
        p = 0.4 * (e - 0.5 * (m[0] * u[0] + m[1] * u[1] + m[2] * u[2]))
        for k in range(3):
            xp[k, i + 3] = u[k]
            mt[k, i] = m[k]
        xp[3, i + 3] = p * inv
        pt[i] = p
        ept[i] = e + p
        return 0

    for load in loads[:3]:
        load.wait()
    edges = sorted({*range(3), *range(lx - 3, lx)})
    for i in edges:
        primitives(i)

    zeros3 = jnp.zeros((3, lz, ly), jnp.float32)

    def x_halo(ref, fields, base):
        to_next = pltpu.make_async_remote_copy(
            ref.at[:, pl.ds(lx, 3)], ref.at[:, pl.ds(0, 3)], hss.at[base], hrs.at[base],
            device_id={"gx": ix + 1}, device_id_type=MESH)
        to_prev = pltpu.make_async_remote_copy(
            ref.at[:, pl.ds(3, 3)], ref.at[:, pl.ds(lx + 3, 3)], hss.at[base + 1], hrs.at[base + 1],
            device_id={"gx": ix - 1}, device_id_type=MESH)

        @pl.when(ix == 0)
        def _():
            for f in range(fields):
                ref[f, 0:3] = zeros3

        @pl.when(ix == nx - 1)
        def _():
            for f in range(fields):
                ref[f, lx + 3 : lx + 6] = zeros3

        return to_next, to_prev, ix, nx

    def y_halo(source, ref, base):
        to_next = pltpu.make_async_remote_copy(
            source.at[pl.ds(16, 16)], ref.at[pl.ds(0, 16)], hss.at[base], hrs.at[base],
            device_id={"gy": iy + 1}, device_id_type=MESH)
        to_prev = pltpu.make_async_remote_copy(
            source.at[pl.ds(0, 16)], ref.at[pl.ds(16, 16)], hss.at[base + 1], hrs.at[base + 1],
            device_id={"gy": iy - 1}, device_id_type=MESH)

        @pl.when(iy == 0)
        def _():
            ref[0:16] = jnp.zeros((16, rows), jnp.float32)

        @pl.when(iy == ny - 1)
        def _():
            ref[16:32] = jnp.zeros((16, rows), jnp.float32)

        return to_next, to_prev, iy, ny

    def start(halo):
        to_next, to_prev, here, count = halo
        pl.when(here < count - 1)(to_next.start)
        pl.when(here > 0)(to_prev.start)

    def arrive(halo):
        to_next, to_prev, here, count = halo
        pl.when(here > 0)(to_next.wait_recv)
        pl.when(here < count - 1)(to_prev.wait_recv)

    def sent(halo):
        to_next, to_prev, here, count = halo
        pl.when(here < count - 1)(to_next.wait_send)
        pl.when(here > 0)(to_prev.wait_send)

    def packed(field, fields):
        total = None
        for f in range(fields):
            s = part("sel", f)
            p = dot(jnp.concatenate([s, s], 1), two(flat(field(f)), 1), NT)
            total = p if total is None else total + p
        return total

    def pairs(count):
        return [tuple(range(f, min(f + 2, count))) for f in range(0, count, 2)]

    h1x = x_halo(xp, 4, 0)
    lax.fori_loop(3, lx - 3, primitives, 0, unroll=2)
    for load in loads[3:]:
        load.wait()
    ysend[...] = packed(lambda f: xp[f, 3 : lx + 3], 4)
    h1y = y_halo(ysend, yhalo, 2)
    pl.semaphore_wait(barrier, nx + ny - 2)
    start(h1x)
    start(h1y)
    for f in range(4):
        gy[f] = block(dot(two(flat(xp[f, 3 : lx + 3]), 1), part("dy"), NN))
    arrive(h1y)
    outer = two(yhalo[...], 0)
    for fs in pairs(4):
        near = dot(outer, jnp.concatenate([part("ed", f) for f in fs], 1), TN)
        for n, f in enumerate(fs):
            gy[f] += block(near[:, n * ly : n * ly + ly])

    def fluxes(i, _=None):
        u = [xp[k, i + 3] for k in range(3)]
        m = [mt[k, i] for k in range(3)]
        p, ep = pt[i], ept[i]
        g = [
            [difference(lambda k: xp[f, i + 3 + k]) for f in range(4)],
            [gy[f, i] for f in range(4)],
            [around(xp[f, i + 3]) for f in range(4)],
        ]
        dilation = (2.0 / 3.0 * viscosity * STEP) * (g[0][0] + g[1][1] + g[2][2])
        stress = {}
        for a in range(3):
            for b in range(a, 3):
                if a == b:
                    s = (2.0 * viscosity * STEP) * g[a][a] - dilation
                else:
                    s = (viscosity * STEP) * (g[a][b] + g[b][a])
                stress[a, b] = stress[b, a] = s
        for j in range(3):
            entries = [m[j]]
            for k in range(3):
                e = m[k] * u[j] - stress[k, j]
                entries.append(e + p if k == j else e)
            power = u[0] * stress[0, j] + u[1] * stress[1, j] + u[2] * stress[2, j]
            entries.append(ep * u[j] - power - (conductivity * STEP) * g[j][3])
            for c in range(5):
                if j == 0:
                    fxp[c, i + 3] = entries[c]
                elif j == 1:
                    fy[c, i] = entries[c]
                else:
                    dz[c, i] = around(entries[c])
        return 0

    lax.fori_loop(3, lx - 3, fluxes, 0)
    arrive(h1x)
    for i in edges:
        fluxes(i)
    h2x = x_halo(fxp, 5, 4)
    start(h2x)
    ysend2[...] = packed(lambda f: fy[f], 5)
    h2y = y_halo(ysend2, yhalo2, 6)
    start(h2y)

    for f in range(5):
        inner = block(dot(two(flat(fy[f]), 1), part("dy"), NN))
        for i in range(lx):
            s = difference(lambda k: fxp[f, i + 3 + k] if 0 <= i + k < lx else None)
            inc[f, i] = s + dz[f, i] + inner[i]

    width = 32 + 2 * (nx - 1)

    def xtab(k):
        return xt[ix * width + k]

    arrive(h2y)
    outer = two(yhalo2[...], 0)
    for fs in pairs(5):
        near = dot(outer, jnp.concatenate([part("ed", f) for f in fs], 1), TN)
        for n, f in enumerate(fs):
            add = block(near[:, n * ly : n * ly + ly])
            y0 = yl = None
            for i in range(lx):
                s = inc[f, i] + add[i]
                inc[f, i] = s
                a, b = float(scale * xinv[0, i]) * s, float(scale * xinv[-1, i]) * s
                y0, yl = (a, b) if i == 0 else (y0 + a, yl + b)
            first = [fxp[f, 3 + m] for m in range(3)]
            last = [fxp[f, lx + 2 - m] for m in range(3)]
            for w, base in ((0, 0), (1, 8)):
                near_side, far_side = (first, last) if w == 0 else (last, first)
                near_at, far_at = (2, 5) if w == 0 else (5, 2)
                total = xtab(base) * y0 + xtab(base + 1) * yl
                for m in range(3):
                    total += xtab(base + near_at + m) * near_side[m]
                xs[2 + w, f] = total
                for m in range(3):
                    total += xtab(base + far_at + m) * far_side[m]
                xs[w, f] = total
    copies = []
    for d in range(1, nx):
        above, below = (2 if d == 1 else 0), (3 if d == nx - 1 else 1)
        which = jnp.where(ix + d >= nx, below, above).astype(jnp.int32)
        copy = pltpu.make_async_remote_copy(
            xs.at[which], xr.at[d - 1], xss.at[d - 1], xrs.at[d - 1],
            device_id={"gx": lax.rem(ix + d, nx)}, device_id_type=MESH)
        copy.start()
        copies.append(copy)

    arrive(h2x)
    for fs in pairs(5):
        v = {}
        for i in range(lx):
            for f in fs:
                s = inc[f, i]
                if i < 3 or i >= lx - 3:
                    s = s + difference(lambda k: None if 0 <= i + k < lx else fxp[f, i + 3 + k])
                s = float(scale * ipiv[i]) * s
                v[f] = s if i == 0 else s + float(coefficient * ipiv[i]) * v[f]
                inc[f, i] = v[f]
        for i in range(lx - 2, -1, -1):
            for f in fs:
                v[f] = inc[f, i] - float(coefficient * ipiv[i]) * v[f]
                inc[f, i] = v[f]

    edges_y = None
    for f in range(5):
        data = three(flat(inc[f]), 1)
        w = part("wy", f)
        p = dot(jnp.concatenate([w[0:16], w[0:16], w[16:32]], 1), data, NT)
        edges_y = p if edges_y is None else edges_y + p
        fy[f] = block(dot(data, part("inverse"), NN))

    for copy in copies:
        copy.wait_recv()
    outside_x = []
    for f in range(5):
        y0, yl = inc[f, 0], inc[f, lx - 1]
        terms = [y0, yl] + [fxp[f, 3 + m] for m in range(3)] + [fxp[f, lx + 2 - m] for m in range(3)]
        sides = []
        for base in (16, 24):
            total = xtab(base) * terms[0]
            for k in range(1, 8):
                total += xtab(base + k) * terms[k]
            sides.append(total)
        for d in range(1, nx):
            r = xr[d - 1, f]
            sides[0] += xtab(31 + d) * r
            sides[1] += xtab(31 + nx - 1 + d) * r
        outside_x.append(jnp.concatenate(sides, 0))
    small = None
    for f in range(5):
        w = part("wy", f)
        p = dot(jnp.concatenate([w[0:16], w[0:16], w[16:32]], 1), three(outside_x[f], 1), NT)
        small = p if small is None else small + p
    spread = jnp.concatenate([part("spread", c) for c in range(rows // ly)], 1)
    edges_y += dot(three(small, 1), spread, NN)

    ywidth = 8 + 2 * (ny - 1)

    def ytab(k):
        return yt[iy * ywidth + k]

    y0, yl = edges_y[0:8], edges_y[8:16]
    ws[0] = ytab(0) * y0 + ytab(1) * yl
    ws[1] = ytab(2) * y0 + ytab(3) * yl
    ycopies = []
    for d in range(1, ny):
        which = jnp.where(iy + d >= ny, 1, 0).astype(jnp.int32)
        copy = pltpu.make_async_remote_copy(
            ws.at[which], wr.at[d - 1], wss.at[d - 1], wrs.at[d - 1],
            device_id={"gy": lax.rem(iy + d, ny)}, device_id_type=MESH)
        copy.start()
        ycopies.append(copy)
    solved = dot(three(jnp.concatenate(outside_x, 0), 1), part("inverse"), NN)
    for f in range(5):
        low, high = solved[2 * lz * f : 2 * lz * f + lz], solved[2 * lz * f + lz : 2 * lz * (f + 1)]
        for i in range(lx):
            at = pl.ds(i, lz, stride=lx)
            state = mass[at, :] if f == 0 else (energy[at, :] if f == 4 else mt[f - 1, i])
            inc[f, i] = state + fy[f, i] + float(alpha[i]) * low + float(beta[i]) * high
    before = ytab(4) * y0 + ytab(5) * yl
    after = ytab(6) * y0 + ytab(7) * yl
    for d in range(1, ny):
        ycopies[d - 1].wait_recv()
        r = wr[d - 1]
        before += ytab(7 + d) * r
        after += ytab(7 + ny - 1 + d) * r
    outside = three(jnp.concatenate([before, after], 0), 0)
    for fs in pairs(5):
        far = dot(outside, jnp.concatenate([part("ey", f) for f in fs], 1), TN)
        for n, f in enumerate(fs):
            total = block(far[:, n * ly : n * ly + ly])
            for i in range(lx):
                out[f, pl.ds(i, lz, stride=lx), :] = inc[f, i] + total[i]

    for halo in (h1x, h1y, h2x, h2y):
        sent(halo)
    for copy in copies + ycopies:
        copy.wait_send()


def body(nx, ny, mass, mom, energy):
    lz, lx, ly = mass.shape
    rows = lx * lz
    coefficient = float(max(lx, ly))
    xtab, xinv, xa, xb = coupled_tables(lx, nx, coefficient, -2.0 * coefficient * STEP)
    ytab, ya, yb = reduced_tables(ly, ny, coefficient)
    tab, places = lane_tables(lx, lz, ly, coefficient, xa, xb, ya, yb)
    vm = pl.BlockSpec(memory_space=pltpu.VMEM)
    hbm = pl.BlockSpec(memory_space=pltpu.HBM)
    f32 = jnp.float32
    block = (lx, lz, ly)
    dma = pltpu.SemaphoreType.DMA
    operands = (
        mass.reshape(rows, ly), mom.reshape(3, rows, ly), energy.reshape(rows, ly),
        jnp.asarray(tab), jnp.asarray(xtab.reshape(-1)), jnp.asarray(ytab.reshape(-1)),
    )
    result = pl.pallas_call(
        functools.partial(
            kernel, nx, ny, lx, lz, ly, coefficient, pivots(lx, coefficient), xinv, xa, xb, places),
        out_shape=jax.ShapeDtypeStruct((5, rows, ly), f32),
        in_specs=[hbm] * 6,
        out_specs=vm,
        scratch_shapes=[
            pltpu.VMEM((rows, ly), f32),
            pltpu.VMEM((3, rows, ly), f32),
            pltpu.VMEM((rows, ly), f32),
            pltpu.VMEM(tab.shape, jnp.bfloat16),
            pltpu.SMEM((xtab.size,), f32),
            pltpu.SMEM((ytab.size,), f32),
            pltpu.VMEM((4, lx + 6, lz, ly), f32),
            pltpu.VMEM(block, f32),
            pltpu.VMEM(block, f32),
            pltpu.VMEM((3, *block), f32),
            pltpu.VMEM((4, *block), f32),
            pltpu.VMEM((5, lx + 6, lz, ly), f32),
            pltpu.VMEM((5, *block), f32),
            pltpu.VMEM((5, *block), f32),
            pltpu.VMEM((5, *block), f32),
            pltpu.VMEM((32, rows), f32),
            pltpu.VMEM((32, rows), f32),
            pltpu.VMEM((32, rows), f32),
            pltpu.VMEM((32, rows), f32),
            pltpu.VMEM((4, 5, lz, ly), f32),
            pltpu.VMEM((nx - 1, 5, lz, ly), f32),
            pltpu.VMEM((2, 8, rows), f32),
            pltpu.VMEM((ny - 1, 8, rows), f32),
            dma((8,)),
            dma((8,)),
            dma((nx - 1,)),
            dma((nx - 1,)),
            dma((ny - 1,)),
            dma((ny - 1,)),
            dma((6,)),
        ],
        compiler_params=pltpu.CompilerParams(
            collective_id=0, has_side_effects=True, vmem_limit_bytes=40 * 2**20
        ),
    )(*[pltpu.with_memory_space_constraint(a, pltpu.HBM) for a in operands])
    return result.reshape(5, lz, lx, ly)


def solution(mesh):
    return jax.shard_map(
        functools.partial(body, mesh.shape["gx"], mesh.shape["gy"]),
        mesh=mesh,
        in_specs=(P(None, "gx", "gy"), P(None, None, "gx", "gy"), P(None, "gx", "gy")),
        out_specs=P(None, None, "gx", "gy"),
        check_vma=False,
    )
```

time: 37.4 us -> 29.5 us (0.79)
  Pallas kernels: 35.8 us -> 27.9 us
    pallas_call x1, Pallas kernels: 35.8 us -> 27.9 us  [body(): pl.pallas_call(functools.partial(kernel, nx, ny, lx, lz, ly, coefficient,...]
where the time goes in v2:
time: 29.5 us; the launch traced here: 29 us
  Pallas kernels  27.9 us (95%)
  local copies, waits for them, and re-layouts  1.06 us (4%)
    pallas_call x1, Pallas kernels, body(): pl.pallas_call(functools.partial(kernel, nx, ny, lx, lz, ly, coefficient,...  27.9 us
    unnamed x1, local copies, waits for them, and re-layouts  1.06 us

profile of v2, /device:TPU:1, one launch (start us, length us, event | category | flops | bytes accessed | tf_op | source)
XLA Modules:
  0.0 29.0 jit_solution(6146818291562126678)
XLA Ops:
  0.0 27.9 %shard_map.64 = f32[5,512,128]{2,1,0:T(8,128)S(1)} custom-call(f32[512,128]{1,0:T(8,128)} %bitcast.6, f32[3,512,128]{2,1,0:T(8,128)} %bitcast.5, f32[512,128]{1,0:T(8,128)} %bitcast.7, bf16[1904,128]{1,0:T(8,128)(2,1)} %constant.6.clone.tab_in, f32[368]{0:T(512)} %constant.7.clone.xt_in, f32[56]{0:T(128)} %constant.8.clone.yt_in), custom_call_target="tpu_custom_call" | custom-call | tf_op jit(solution)/shard_map/pallas_call | solution.py:556
  27.9 1.1 %copy.8 = f32[5,16,32,128]{3,2,1,0:T(8,128)} copy(f32[5,16,32,128]{3,2,1,0:T(8,128)S(1)} %bitcast.4) | data formatting | bytes 2621440

commit v3 on v2

--- a/solution.py
+++ b/solution.py
@@ -219,16 +219,41 @@
     mass_in, mom_in, energy_in, tab_in, xt_in, yt_in, out,
     mass, mom, energy, tab, xt, yt,
     xp, pt, ept, mt, gy, fxp, fy, dz, inc, ysend, yhalo, ysend2, yhalo2,
-    xs, xr, ws, wr,
-    hss, hrs, xss, xrs, wss, wrs, lsem,
+    xs, xl, xr, ws, wr, vs, vr, cs, cr,
+    hss, hrs, xss, xrs, wss, wrs, vss, vrs, css, crs, lsem, near_sem,
 ):
     ix, iy = lax.axis_index("gx"), lax.axis_index("gy")
     rows = lx * lz
     scale = -2.0 * coefficient * STEP
 
     barrier = pltpu.get_barrier_semaphore()
-    for d in range(1, nx):
-        pl.semaphore_signal(barrier, inc=1, device_id={"gx": lax.rem(ix + d, nx)}, device_id_type=MESH)
+
+
+    def both_sides(semaphore, distance):
+        above, below = ix + distance < nx, ix - distance >= 0
+
+        @pl.when(above)
+        def _():
+            pl.semaphore_signal(semaphore, inc=1, device_id={"gx": ix + distance}, device_id_type=MESH)
+
+        @pl.when(below)
+        def _():
+            pl.semaphore_signal(semaphore, inc=1, device_id={"gx": ix - distance}, device_id_type=MESH)
+
+        return above.astype(jnp.int32) + below.astype(jnp.int32)
+
+    expected = both_sides(barrier, 1)
+    stages = []
+
+    def tell():
+        distance = 1 << len(stages)
+        if distance < nx - 1:
+            stages.append(both_sides(near_sem.at[len(stages)], distance))
+
+    def hear():
+        if stages and stages[-1] is not None:
+            pl.semaphore_wait(near_sem.at[len(stages) - 1], stages[-1])
+
     for d in range(1, ny):
         pl.semaphore_signal(barrier, inc=1, device_id={"gy": lax.rem(iy + d, ny)}, device_id_type=MESH)
 
@@ -343,12 +368,15 @@
         load.wait()
     ysend[...] = packed(lambda f: xp[f, 3 : lx + 3], 4)
     h1y = y_halo(ysend, yhalo, 2)
-    pl.semaphore_wait(barrier, nx + ny - 2)
+    pl.semaphore_wait(barrier, expected + (ny - 1))
     start(h1x)
     start(h1y)
+    tell()
     for f in range(4):
         gy[f] = block(dot(two(flat(xp[f, 3 : lx + 3]), 1), part("dy"), NN))
     arrive(h1y)
+    hear()
+    tell()
     outer = two(yhalo[...], 0)
     for fs in pairs(4):
         near = dot(outer, jnp.concatenate([part("ed", f) for f in fs], 1), TN)
@@ -391,6 +419,8 @@
 
     lax.fori_loop(3, lx - 3, fluxes, 0)
     arrive(h1x)
+    hear()
+    tell()
     for i in edges:
         fluxes(i)
     h2x = x_halo(fxp, 5, 4)
@@ -434,15 +464,80 @@
                 for m in range(3):
                     total += xtab(base + far_at + m) * far_side[m]
                 xs[w, f] = total
+    solved = dot(three(xs[...].reshape(20 * lz, ly), 1), part("inverse"), NN)
+    xl[...] = solved.reshape(4, 5, lz, ly)
+    hear()
+    while (1 << len(stages)) < nx - 1:
+        tell()
+        hear()
     copies = []
     for d in range(1, nx):
         above, below = (2 if d == 1 else 0), (3 if d == nx - 1 else 1)
         which = jnp.where(ix + d >= nx, below, above).astype(jnp.int32)
         copy = pltpu.make_async_remote_copy(
-            xs.at[which], xr.at[d - 1], xss.at[d - 1], xrs.at[d - 1],
+            xl.at[which], xr.at[d - 1], xss.at[d - 1], xrs.at[d - 1],
             device_id={"gx": lax.rem(ix + d, nx)}, device_id_type=MESH)
         copy.start()
         copies.append(copy)
+
+    ywidth = 8 + 2 * (ny - 1)
+
+    def ytab(k):
+        return yt[iy * ywidth + k]
+
+    def ends(data, f):
+        w = part("wy", f)
+        return dot(jnp.concatenate([w[0:16], w[0:16], w[16:32]], 1), data, NT)
+
+    def y_exchange(values, source, target, send, receive):
+        y0, yl = values[0:8], values[8:16]
+        source[0] = ytab(0) * y0 + ytab(1) * yl
+        source[1] = ytab(2) * y0 + ytab(3) * yl
+        started = []
+        for d in range(1, ny):
+            which = jnp.where(iy + d >= ny, 1, 0).astype(jnp.int32)
+            copy = pltpu.make_async_remote_copy(
+                source.at[which], target.at[d - 1], send.at[d - 1], receive.at[d - 1],
+                device_id={"gy": lax.rem(iy + d, ny)}, device_id_type=MESH)
+            copy.start()
+            started.append(copy)
+
+        def finish():
+            before = ytab(4) * y0 + ytab(5) * yl
+            after = ytab(6) * y0 + ytab(7) * yl
+            for d in range(1, ny):
+                started[d - 1].wait_recv()
+                r = target[d - 1]
+                before += ytab(7 + d) * r
+                after += ytab(7 + ny - 1 + d) * r
+            return before, after
+
+        return started, finish
+
+    values = None
+    spare = jnp.zeros((ly - 4 * lz, ly), jnp.float32)
+    for f in range(5):
+        p = ends(three(jnp.concatenate([xs[:, f].reshape(4 * lz, ly), spare], 0), 1), f)
+        values = p if values is None else values + p
+    vcopies, finish = y_exchange(values, vs, vr, vss, vrs)
+    before, after = finish()
+    lane = lax.broadcasted_iota(jnp.int32, (8, ly), 1)
+
+    def shifted(v, by):
+        return pltpu.roll(v, by % ly, 1) if by % ly else v
+
+    for w in range(4):
+        low, high = shifted(before, -lz * w), shifted(after, lz - lz * w)
+        cs[w] = jnp.where(lane < lz, low, jnp.where(lane < 2 * lz, high, 0.0))
+    ccopies = []
+    for d in range(1, nx):
+        above, below = (2 if d == 1 else 0), (3 if d == nx - 1 else 1)
+        which = jnp.where(ix + d >= nx, below, above).astype(jnp.int32)
+        copy = pltpu.make_async_remote_copy(
+            cs.at[which], cr.at[d - 1], css.at[d - 1], crs.at[d - 1],
+            device_id={"gx": lax.rem(ix + d, nx)}, device_id_type=MESH)
+        copy.start()
+        ccopies.append(copy)
 
     arrive(h2x)
     for fs in pairs(5):
@@ -460,17 +555,7 @@
                 v[f] = inc[f, i] - float(coefficient * ipiv[i]) * v[f]
                 inc[f, i] = v[f]
 
-    edges_y = None
-    for f in range(5):
-        data = three(flat(inc[f]), 1)
-        w = part("wy", f)
-        p = dot(jnp.concatenate([w[0:16], w[0:16], w[16:32]], 1), data, NT)
-        edges_y = p if edges_y is None else edges_y + p
-        fy[f] = block(dot(data, part("inverse"), NN))
-
-    for copy in copies:
-        copy.wait_recv()
-    outside_x = []
+    own_x = []
     for f in range(5):
         y0, yl = inc[f, 0], inc[f, lx - 1]
         terms = [y0, yl] + [fxp[f, 3 + m] for m in range(3)] + [fxp[f, lx + 2 - m] for m in range(3)]
@@ -480,60 +565,59 @@
             for k in range(1, 8):
                 total += xtab(base + k) * terms[k]
             sides.append(total)
-        for d in range(1, nx):
-            r = xr[d - 1, f]
-            sides[0] += xtab(31 + d) * r
-            sides[1] += xtab(31 + nx - 1 + d) * r
-        outside_x.append(jnp.concatenate(sides, 0))
-    small = None
+        own_x.append(jnp.concatenate(sides, 0))
+
+    values = small = None
     for f in range(5):
-        w = part("wy", f)
-        p = dot(jnp.concatenate([w[0:16], w[0:16], w[16:32]], 1), three(outside_x[f], 1), NT)
+        data = three(flat(inc[f]), 1)
+        p = ends(data, f)
+        values = p if values is None else values + p
+        fy[f] = block(dot(data, part("inverse"), NN))
+        p = ends(three(own_x[f], 1), f)
         small = p if small is None else small + p
     spread = jnp.concatenate([part("spread", c) for c in range(rows // ly)], 1)
-    edges_y += dot(three(small, 1), spread, NN)
-
-    ywidth = 8 + 2 * (ny - 1)
-
-    def ytab(k):
-        return yt[iy * ywidth + k]
-
-    y0, yl = edges_y[0:8], edges_y[8:16]
-    ws[0] = ytab(0) * y0 + ytab(1) * yl
-    ws[1] = ytab(2) * y0 + ytab(3) * yl
-    ycopies = []
-    for d in range(1, ny):
-        which = jnp.where(iy + d >= ny, 1, 0).astype(jnp.int32)
-        copy = pltpu.make_async_remote_copy(
-            ws.at[which], wr.at[d - 1], wss.at[d - 1], wrs.at[d - 1],
-            device_id={"gy": lax.rem(iy + d, ny)}, device_id_type=MESH)
-        copy.start()
-        ycopies.append(copy)
-    solved = dot(three(jnp.concatenate(outside_x, 0), 1), part("inverse"), NN)
+    values += dot(three(small, 1), spread, NN)
+    ycopies, finish = y_exchange(values, ws, wr, wss, wrs)
+    solved = dot(three(jnp.concatenate(own_x, 0), 1), part("inverse"), NN)
     for f in range(5):
         low, high = solved[2 * lz * f : 2 * lz * f + lz], solved[2 * lz * f + lz : 2 * lz * (f + 1)]
         for i in range(lx):
             at = pl.ds(i, lz, stride=lx)
             state = mass[at, :] if f == 0 else (energy[at, :] if f == 4 else mt[f - 1, i])
             inc[f, i] = state + fy[f, i] + float(alpha[i]) * low + float(beta[i]) * high
-    before = ytab(4) * y0 + ytab(5) * yl
-    after = ytab(6) * y0 + ytab(7) * yl
-    for d in range(1, ny):
-        ycopies[d - 1].wait_recv()
-        r = wr[d - 1]
-        before += ytab(7 + d) * r
-        after += ytab(7 + ny - 1 + d) * r
-    outside = three(jnp.concatenate([before, after], 0), 0)
+    outside = three(jnp.concatenate(finish(), 0), 0)
     for fs in pairs(5):
         far = dot(outside, jnp.concatenate([part("ey", f) for f in fs], 1), TN)
         for n, f in enumerate(fs):
-            total = block(far[:, n * ly : n * ly + ly])
+            inc[f] += block(far[:, n * ly : n * ly + ly])
+
+    for copy in ccopies:
+        copy.wait_recv()
+    sides = []
+    for at in (31, 31 + nx - 1):
+        total = xtab(at + 1) * cr[0]
+        for d in range(2, nx):
+            total += xtab(at + d) * cr[d - 1]
+        sides.append(jnp.concatenate([total, shifted(total, -lz)], 0))
+    lane = lax.broadcasted_iota(jnp.int32, (16, ly), 1)
+    outside = three(jnp.where(lane < lz, sides[0], jnp.where(lane < 2 * lz, shifted(sides[1], lz), 0.0)), 0)
+    for copy in copies:
+        copy.wait_recv()
+    for fs in pairs(5):
+        far = dot(outside, jnp.concatenate([part("ey", f) for f in fs], 1), TN)
+        for n, f in enumerate(fs):
+            low = far[0:lz, n * ly : n * ly + ly]
+            high = far[lz : 2 * lz, n * ly : n * ly + ly]
+            for d in range(1, nx):
+                r = xr[d - 1, f]
+                low += xtab(31 + d) * r
+                high += xtab(31 + nx - 1 + d) * r
             for i in range(lx):
-                out[f, pl.ds(i, lz, stride=lx), :] = inc[f, i] + total[i]
+                out[f, pl.ds(i, lz, stride=lx), :] = inc[f, i] + float(alpha[i]) * low + float(beta[i]) * high
 
     for halo in (h1x, h1y, h2x, h2y):
         sent(halo)
-    for copy in copies + ycopies:
+    for copy in copies + ccopies + vcopies + ycopies:
         copy.wait_send()
 
 
@@ -580,16 +664,26 @@
             pltpu.VMEM((32, rows), f32),
             pltpu.VMEM((32, rows), f32),
             pltpu.VMEM((4, 5, lz, ly), f32),
+            pltpu.VMEM((4, 5, lz, ly), f32),
             pltpu.VMEM((nx - 1, 5, lz, ly), f32),
             pltpu.VMEM((2, 8, rows), f32),
             pltpu.VMEM((ny - 1, 8, rows), f32),
+            pltpu.VMEM((2, 8, ly), f32),
+            pltpu.VMEM((ny - 1, 8, ly), f32),
+            pltpu.VMEM((4, 8, ly), f32),
+            pltpu.VMEM((nx - 1, 8, ly), f32),
             dma((8,)),
             dma((8,)),
             dma((nx - 1,)),
             dma((nx - 1,)),
             dma((ny - 1,)),
             dma((ny - 1,)),
+            dma((ny - 1,)),
+            dma((ny - 1,)),
+            dma((nx - 1,)),
+            dma((nx - 1,)),
             dma((6,)),
+            pltpu.SemaphoreType.REGULAR((max(1, (nx - 1).bit_length()),)),
         ],
         compiler_params=pltpu.CompilerParams(
             collective_id=0, has_side_effects=True, vmem_limit_bytes=40 * 2**20

time: 29.5 us -> 27.6 us (0.936); the launches traced: 29 us -> 27.5 us
  Pallas kernels: 27.9 us -> 26.4 us
    pallas_call x1, Pallas kernels: 27.9 us -> 26.4 us  [body(): pl.pallas_call(functools.partial(kernel, nx, ny, lx, lz, ly, coefficient,...]
where the time goes in v3:
time: 27.6 us; the launch traced here: 27.5 us
  Pallas kernels  26.4 us (96%)
  local copies, waits for them, and re-layouts  1.06 us (4%)
    pallas_call x1, Pallas kernels, body(): pl.pallas_call(functools.partial(kernel, nx, ny, lx, lz, ly, coefficient,...  26.4 us
    unnamed x1, local copies, waits for them, and re-layouts  1.06 us

profile of v3, /device:TPU:1, one launch (start us, length us, event | category | flops | bytes accessed | tf_op | source)
XLA Modules:
  0.0 27.5 jit_solution(478752618636206363)
XLA Ops:
  0.0 26.4 %shard_map.64 = f32[5,512,128]{2,1,0:T(8,128)S(1)} custom-call(f32[512,128]{1,0:T(8,128)} %bitcast.6, f32[3,512,128]{2,1,0:T(8,128)} %bitcast.5, f32[512,128]{1,0:T(8,128)} %bitcast.7, bf16[1904,128]{1,0:T(8,128)(2,1)} %constant.6.clone.tab_in, f32[368]{0:T(512)} %constant.7.clone.xt_in, f32[56]{0:T(128)} %constant.8.clone.yt_in), custom_call_target="tpu_custom_call" | custom-call | tf_op jit(solution)/shard_map/pallas_call | solution.py:640
  26.4 1.1 %copy.8 = f32[5,16,32,128]{3,2,1,0:T(8,128)} copy(f32[5,16,32,128]{3,2,1,0:T(8,128)S(1)} %bitcast.4) | data formatting | bytes 2621440

commit v4 on v3

--- a/solution.py
+++ b/solution.py
@@ -129,7 +129,7 @@
     return high.astype(np.float64), low.astype(np.float64)
 
 
-def lane_tables(lx, lz, ly, coefficient, xa, xb, ya, yb):
+def lane_tables(lx, lz, ly, coefficient, xinv, xa, xb, ya, yb):
     inverse = local_inverse(ly, coefficient)
     dy = np.zeros((ly, ly))
     for j in range(ly):
@@ -150,10 +150,12 @@
                         ed[f, row, position - step] = w
         wy[f, f], wy[f, 8 + f] = inverse[0], inverse[-1]
         ey[f, f], ey[f, 8 + f] = ya, yb
-    spread = np.zeros((2, lz, lx, lz))
-    for z in range(lz):
-        spread[0, z, :, z], spread[1, z, :, z] = xa, xb
-    spread = spread.reshape(2 * lz, lx * lz)
+    profiles = [xa, xb, *(xinv[:, r] for r in (*range(3), *range(lx - 3, lx)))]
+    spread = np.zeros((8, lz, lx, lz))
+    for n, profile in enumerate(profiles):
+        for z in range(lz):
+            spread[n, z, :, z] = profile
+    spread = spread.reshape(8 * lz, lx * lz)
     parts = {"dy": np.concatenate([dy, dy])}
     high, low = halves(inverse.T)
     parts["inverse"] = np.concatenate([high, high, low])
@@ -216,9 +218,9 @@
 
 def kernel(
     nx, ny, lx, lz, ly, coefficient, ipiv, xinv, alpha, beta, places,
-    mass_in, mom_in, energy_in, tab_in, xt_in, yt_in, out,
+    mass_in, mom_in, energy_in, tab_in, xt_in, yt_in, out, low_out, high_out,
     mass, mom, energy, tab, xt, yt,
-    xp, pt, ept, mt, gy, fxp, fy, dz, inc, ysend, yhalo, ysend2, yhalo2,
+    xp, pt, ept, mt, gy, pre, fxp, fy, dz, inc, ysend, yhalo, ysend2, yhalo2,
     xs, xl, xr, ws, wr, vs, vr, cs, cr,
     hss, hrs, xss, xrs, wss, wrs, vss, vrs, css, crs, lsem, near_sem,
 ):
@@ -363,17 +365,29 @@
         return [tuple(range(f, min(f + 2, count))) for f in range(0, count, 2)]
 
     h1x = x_halo(xp, 4, 0)
+    pl.semaphore_wait(barrier, expected + (ny - 1))
+    start(h1x)
+    tell()
     lax.fori_loop(3, lx - 3, primitives, 0, unroll=2)
     for load in loads[3:]:
         load.wait()
     ysend[...] = packed(lambda f: xp[f, 3 : lx + 3], 4)
     h1y = y_halo(ysend, yhalo, 2)
-    pl.semaphore_wait(barrier, expected + (ny - 1))
-    start(h1x)
     start(h1y)
-    tell()
     for f in range(4):
         gy[f] = block(dot(two(flat(xp[f, 3 : lx + 3]), 1), part("dy"), NN))
+
+    def gradients(i):
+        x = [difference(lambda k: xp[f, i + 3 + k]) for f in range(4)]
+        z = [around(xp[f, i + 3]) for f in range(4)]
+        return x[0], z[2], x[1], x[2] + z[0], z[1], x[3], z[3]
+
+    def ahead(i, _=None):
+        for n, g in enumerate(gradients(i)):
+            pre[n, i] = g
+        return 0
+
+    lax.fori_loop(3, lx - 3, ahead, 0, unroll=2)
     arrive(h1y)
     hear()
     tell()
@@ -383,31 +397,28 @@
         for n, f in enumerate(fs):
             gy[f] += block(near[:, n * ly : n * ly + ly])
 
-    def fluxes(i, _=None):
+    def fluxes(i, g=None):
         u = [xp[k, i + 3] for k in range(3)]
         m = [mt[k, i] for k in range(3)]
         p, ep = pt[i], ept[i]
-        g = [
-            [difference(lambda k: xp[f, i + 3 + k]) for f in range(4)],
-            [gy[f, i] for f in range(4)],
-            [around(xp[f, i + 3]) for f in range(4)],
-        ]
-        dilation = (2.0 / 3.0 * viscosity * STEP) * (g[0][0] + g[1][1] + g[2][2])
-        stress = {}
-        for a in range(3):
-            for b in range(a, 3):
-                if a == b:
-                    s = (2.0 * viscosity * STEP) * g[a][a] - dilation
-                else:
-                    s = (viscosity * STEP) * (g[a][b] + g[b][a])
-                stress[a, b] = stress[b, a] = s
+        xx, zz, xv, xz, zv, xt, zt = g or [pre[n, i] for n in range(7)]
+        yu, yy, yw, yt = [gy[f, i] for f in range(4)]
+        dilation = (2.0 / 3.0 * viscosity * STEP) * (xx + yy + zz)
+        twice, once = 2.0 * viscosity * STEP, viscosity * STEP
+        stress = {
+            (0, 0): twice * xx - dilation, (1, 1): twice * yy - dilation, (2, 2): twice * zz - dilation,
+            (0, 1): once * (xv + yu), (0, 2): once * xz, (1, 2): once * (yw + zv),
+        }
+        for a, b in ((0, 1), (0, 2), (1, 2)):
+            stress[b, a] = stress[a, b]
+        heat = (xt, yt, zt)
         for j in range(3):
             entries = [m[j]]
             for k in range(3):
                 e = m[k] * u[j] - stress[k, j]
                 entries.append(e + p if k == j else e)
             power = u[0] * stress[0, j] + u[1] * stress[1, j] + u[2] * stress[2, j]
-            entries.append(ep * u[j] - power - (conductivity * STEP) * g[j][3])
+            entries.append(ep * u[j] - power - (conductivity * STEP) * heat[j])
             for c in range(5):
                 if j == 0:
                     fxp[c, i + 3] = entries[c]
@@ -417,12 +428,15 @@
                     dz[c, i] = around(entries[c])
         return 0
 
-    lax.fori_loop(3, lx - 3, fluxes, 0)
+    def inner(i, _):
+        return fluxes(i)
+
+    lax.fori_loop(3, lx - 3, inner, 0)
     arrive(h1x)
     hear()
     tell()
     for i in edges:
-        fluxes(i)
+        fluxes(i, gradients(i))
     h2x = x_halo(fxp, 5, 4)
     start(h2x)
     ysend2[...] = packed(lambda f: fy[f], 5)
@@ -520,6 +534,23 @@
         p = ends(three(jnp.concatenate([xs[:, f].reshape(4 * lz, ly), spare], 0), 1), f)
         values = p if values is None else values + p
     vcopies, finish = y_exchange(values, vs, vr, vss, vrs)
+    for fs in pairs(5):
+        v = {}
+        for i in range(lx):
+            for f in fs:
+                s = float(scale * ipiv[i]) * inc[f, i]
+                v[f] = s if i == 0 else s + float(coefficient * ipiv[i]) * v[f]
+                inc[f, i] = v[f]
+        for i in range(lx - 2, -1, -1):
+            for f in fs:
+                v[f] = inc[f, i] - float(coefficient * ipiv[i]) * v[f]
+                inc[f, i] = v[f]
+    local = None
+    for f in range(5):
+        data = three(flat(inc[f]), 1)
+        p = ends(data, f)
+        local = p if local is None else local + p
+        fy[f] = block(dot(data, part("inverse"), NN))
     before, after = finish()
     lane = lax.broadcasted_iota(jnp.int32, (8, ly), 1)
 
@@ -540,24 +571,17 @@
         ccopies.append(copy)
 
     arrive(h2x)
-    for fs in pairs(5):
-        v = {}
-        for i in range(lx):
-            for f in fs:
-                s = inc[f, i]
-                if i < 3 or i >= lx - 3:
-                    s = s + difference(lambda k: None if 0 <= i + k < lx else fxp[f, i + 3 + k])
-                s = float(scale * ipiv[i]) * s
-                v[f] = s if i == 0 else s + float(coefficient * ipiv[i]) * v[f]
-                inc[f, i] = v[f]
-        for i in range(lx - 2, -1, -1):
-            for f in fs:
-                v[f] = inc[f, i] - float(coefficient * ipiv[i]) * v[f]
-                inc[f, i] = v[f]
-
+    halo_rows = [*range(3), *range(lx - 3, lx)]
     own_x = []
+    small = None
     for f in range(5):
+        added = []
+        for i in halo_rows:
+            added.append(scale * difference(lambda k: None if 0 <= i + k < lx else fxp[f, i + 3 + k]))
         y0, yl = inc[f, 0], inc[f, lx - 1]
+        for i, v in zip(halo_rows, added):
+            y0 += float(xinv[0, i]) * v
+            yl += float(xinv[-1, i]) * v
         terms = [y0, yl] + [fxp[f, 3 + m] for m in range(3)] + [fxp[f, lx + 2 - m] for m in range(3)]
         sides = []
         for base in (16, 24):
@@ -565,31 +589,29 @@
             for k in range(1, 8):
                 total += xtab(base + k) * terms[k]
             sides.append(total)
-        own_x.append(jnp.concatenate(sides, 0))
-
-    values = small = None
-    for f in range(5):
-        data = three(flat(inc[f]), 1)
-        p = ends(data, f)
-        values = p if values is None else values + p
-        fy[f] = block(dot(data, part("inverse"), NN))
+        own_x.append(jnp.concatenate(sides + added, 0))
         p = ends(three(own_x[f], 1), f)
         small = p if small is None else small + p
     spread = jnp.concatenate([part("spread", c) for c in range(rows // ly)], 1)
-    values += dot(three(small, 1), spread, NN)
-    ycopies, finish = y_exchange(values, ws, wr, wss, wrs)
+    ycopies, finish = y_exchange(local + dot(three(small, 1), spread, NN), ws, wr, wss, wrs)
     solved = dot(three(jnp.concatenate(own_x, 0), 1), part("inverse"), NN)
     for f in range(5):
-        low, high = solved[2 * lz * f : 2 * lz * f + lz], solved[2 * lz * f + lz : 2 * lz * (f + 1)]
+        pieces = [solved[lz * (8 * f + n) : lz * (8 * f + n + 1)] for n in range(8)]
         for i in range(lx):
             at = pl.ds(i, lz, stride=lx)
             state = mass[at, :] if f == 0 else (energy[at, :] if f == 4 else mt[f - 1, i])
-            inc[f, i] = state + fy[f, i] + float(alpha[i]) * low + float(beta[i]) * high
+            total = state + fy[f, i]
+            weights = [alpha[i], beta[i], *(xinv[i, r] for r in halo_rows)]
+            for w, v in zip(weights, pieces):
+                total += float(w) * v
+            inc[f, i] = total
     outside = three(jnp.concatenate(finish(), 0), 0)
     for fs in pairs(5):
         far = dot(outside, jnp.concatenate([part("ey", f) for f in fs], 1), TN)
         for n, f in enumerate(fs):
-            inc[f] += block(far[:, n * ly : n * ly + ly])
+            total = block(far[:, n * ly : n * ly + ly])
+            for i in range(lx):
+                out[f, pl.ds(i, lz, stride=lx), :] = inc[f, i] + total[i]
 
     for copy in ccopies:
         copy.wait_recv()
@@ -612,8 +634,7 @@
                 r = xr[d - 1, f]
                 low += xtab(31 + d) * r
                 high += xtab(31 + nx - 1 + d) * r
-            for i in range(lx):
-                out[f, pl.ds(i, lz, stride=lx), :] = inc[f, i] + float(alpha[i]) * low + float(beta[i]) * high
+            low_out[f], high_out[f] = low, high
 
     for halo in (h1x, h1y, h2x, h2y):
         sent(halo)
@@ -627,7 +648,7 @@
     coefficient = float(max(lx, ly))
     xtab, xinv, xa, xb = coupled_tables(lx, nx, coefficient, -2.0 * coefficient * STEP)
     ytab, ya, yb = reduced_tables(ly, ny, coefficient)
-    tab, places = lane_tables(lx, lz, ly, coefficient, xa, xb, ya, yb)
+    tab, places = lane_tables(lx, lz, ly, coefficient, xinv, xa, xb, ya, yb)
     vm = pl.BlockSpec(memory_space=pltpu.VMEM)
     hbm = pl.BlockSpec(memory_space=pltpu.HBM)
     f32 = jnp.float32
@@ -637,12 +658,12 @@
         mass.reshape(rows, ly), mom.reshape(3, rows, ly), energy.reshape(rows, ly),
         jnp.asarray(tab), jnp.asarray(xtab.reshape(-1)), jnp.asarray(ytab.reshape(-1)),
     )
-    result = pl.pallas_call(
+    result, low, high = pl.pallas_call(
         functools.partial(
             kernel, nx, ny, lx, lz, ly, coefficient, pivots(lx, coefficient), xinv, xa, xb, places),
-        out_shape=jax.ShapeDtypeStruct((5, rows, ly), f32),
+        out_shape=(jax.ShapeDtypeStruct((5, rows, ly), f32), *[jax.ShapeDtypeStruct((5, lz, ly), f32)] * 2),
         in_specs=[hbm] * 6,
-        out_specs=vm,
+        out_specs=(vm, vm, vm),
         scratch_shapes=[
             pltpu.VMEM((rows, ly), f32),
             pltpu.VMEM((3, rows, ly), f32),
@@ -655,6 +676,7 @@
             pltpu.VMEM(block, f32),
             pltpu.VMEM((3, *block), f32),
             pltpu.VMEM((4, *block), f32),
+            pltpu.VMEM((7, *block), f32),
             pltpu.VMEM((5, lx + 6, lz, ly), f32),
             pltpu.VMEM((5, *block), f32),
             pltpu.VMEM((5, *block), f32),
@@ -689,7 +711,9 @@
             collective_id=0, has_side_effects=True, vmem_limit_bytes=40 * 2**20
         ),
     )(*[pltpu.with_memory_space_constraint(a, pltpu.HBM) for a in operands])
-    return result.reshape(5, lz, lx, ly)
+    low, high = low[:, :, None], high[:, :, None]
+    along = [jnp.broadcast_to(jnp.asarray(w.astype(np.float32))[:, None], (lx, ly)) for w in (xa, xb)]
+    return result.reshape(5, lz, lx, ly) + along[0] * low + along[1] * high
 
 
 def solution(mesh):

time: 27.6 us -> 26.5 us (0.960)
  Pallas kernels: 26.4 us -> 24.9 us
  other arithmetic: 0 us -> 1.4 us
  local copies, waits for them, and re-layouts: 1.06 us -> 0.01 us
    pallas_call x1, Pallas kernels: 26.4 us -> 24.9 us  [body(): pl.pallas_call(functools.partial(kernel, nx, ny, lx, lz, ly, coefficient,...]
    add x0 -> x1, other arithmetic: none -> 1.4 us  [body(): return result.reshape(5, lz, lx, ly) + along[0] * low + along[1] * high]
    unnamed x1 -> x4, local copies, waits for them, and re-layouts: 1.06 us -> 0.01 us
where the time goes in v4:
time: 26.5 us; the launch traced here: 26.3 us
  Pallas kernels  24.9 us (94%)
  other arithmetic  1.4 us (5%)
    pallas_call x1, Pallas kernels, body(): pl.pallas_call(functools.partial(kernel, nx, ny, lx, lz, ly, coefficient,...  24.9 us
    add x1, other arithmetic, body(): return result.reshape(5, lz, lx, ly) + along[0] * low + along[1] * high  1.4 us

profile of v4, /device:TPU:1, one launch (start us, length us, event | category | flops | bytes accessed | tf_op | source)
XLA Modules:
  0.0 26.3 jit_solution(5821185881329207955)
XLA Ops:
  0.0 0.0 copy-start
  0.0 0.0 copy-start.1
  0.0 24.9 %shard_map.82 = (f32[5,512,128]{2,1,0:T(8,128)S(1)}, f32[5,16,128]{2,1,0:T(8,128)S(1)}, f32[5,16,128]{2,1,0:T(8,128)S(1)}) custom-call(f32[512,128]{1,0:T(8,128)} %bitcast.6, f32[3,512,128]{2,1,0:T(8,128)} %bitcast.5, f32[512,128]{1,0:T(8,128)} %bitcast.7, bf16[3056,128]{1,0:T(8,128)(2,1)} %constant.10.clone.tab_in, f32[368]{0:T(512)} %constant.11.clone.xt_in, ...), custom_call_target="tpu_custom_call" | custom-call | tf_op jit(solution)/shard_map/pallas_call | solution.py:661
  24.9 0.0 copy-done
  24.9 0.0 copy-done.1
  25.0 1.4 %multiply_add_fusion = f32[5,16,32,128]{3,2,1,0:T(8,128)} fusion(f32[5,16,32,128]{3,2,1,0:T(8,128)S(1)} %bitcast.4, f32[5,16,128]{2,1,0:T(8,128)S(1)} %get-tuple-element.10, f32[32]{0:T(128)S(1)} %copy-done, f32[5,16,128]{2,1,0:T(8,128)S(1)} %get-tuple-element.9, f32[32]{0:T(128)S(1)} %copy-done.1), kind=kLoop, calls=%fused_computation | loop fusion | flops 1310720 | bytes 2703616 | tf_op jit(solution)/shard_map/add | solution.py:716
Async XLA Ops:
  0.0 24.9 %copy-start = (f32[32]{0:T(128)S(1)}, f32[32]{0:T(128)}, u32[]{:S(2)}) copy-start(f32[32]{0:T(128)} %constant.14.clone) | copy-start | bytes 388
  0.0 24.9 %copy-start.1 = (f32[32]{0:T(128)S(1)}, f32[32]{0:T(128)}, u32[]{:S(2)}) copy-start(f32[32]{0:T(128)} %constant.13.clone) | copy-start | bytes 388

commit v5 on v4

--- a/solution.py
+++ b/solution.py
@@ -484,16 +484,6 @@
     while (1 << len(stages)) < nx - 1:
         tell()
         hear()
-    copies = []
-    for d in range(1, nx):
-        above, below = (2 if d == 1 else 0), (3 if d == nx - 1 else 1)
-        which = jnp.where(ix + d >= nx, below, above).astype(jnp.int32)
-        copy = pltpu.make_async_remote_copy(
-            xl.at[which], xr.at[d - 1], xss.at[d - 1], xrs.at[d - 1],
-            device_id={"gx": lax.rem(ix + d, nx)}, device_id_type=MESH)
-        copy.start()
-        copies.append(copy)
-
     ywidth = 8 + 2 * (ny - 1)
 
     def ytab(k):
@@ -533,7 +523,35 @@
     for f in range(5):
         p = ends(three(jnp.concatenate([xs[:, f].reshape(4 * lz, ly), spare], 0), 1), f)
         values = p if values is None else values + p
-    vcopies, finish = y_exchange(values, vs, vr, vss, vrs)
+    lane = lax.broadcasted_iota(jnp.int32, (8, ly), 1)
+
+    def shifted(v, by):
+        return pltpu.roll(v, by % ly, 1) if by % ly else v
+
+    def side_by_side(first, second):
+        return jnp.where(lane < lz, first, jnp.where(lane < 2 * lz, second, 0.0))
+
+    for w in range(4):
+        cs[w] = side_by_side(shifted(values[0:8], -lz * w), shifted(values[8:16], lz - lz * w))
+    ccopies = []
+    for d in range(1, nx):
+        above, below = (2 if d == 1 else 0), (3 if d == nx - 1 else 1)
+        which = jnp.where(ix + d >= nx, below, above).astype(jnp.int32)
+        copy = pltpu.make_async_remote_copy(
+            cs.at[which], cr.at[d - 1], css.at[d - 1], crs.at[d - 1],
+            device_id={"gx": lax.rem(ix + d, nx)}, device_id_type=MESH)
+        copy.start()
+        ccopies.append(copy)
+    copies = []
+    for d in range(1, nx):
+        above, below = (2 if d == 1 else 0), (3 if d == nx - 1 else 1)
+        which = jnp.where(ix + d >= nx, below, above).astype(jnp.int32)
+        copy = pltpu.make_async_remote_copy(
+            xl.at[which], xr.at[d - 1], xss.at[d - 1], xrs.at[d - 1],
+            device_id={"gx": lax.rem(ix + d, nx)}, device_id_type=MESH)
+        copy.start()
+        copies.append(copy)
+
     for fs in pairs(5):
         v = {}
         for i in range(lx):
@@ -551,25 +569,6 @@
         p = ends(data, f)
         local = p if local is None else local + p
         fy[f] = block(dot(data, part("inverse"), NN))
-    before, after = finish()
-    lane = lax.broadcasted_iota(jnp.int32, (8, ly), 1)
-
-    def shifted(v, by):
-        return pltpu.roll(v, by % ly, 1) if by % ly else v
-
-    for w in range(4):
-        low, high = shifted(before, -lz * w), shifted(after, lz - lz * w)
-        cs[w] = jnp.where(lane < lz, low, jnp.where(lane < 2 * lz, high, 0.0))
-    ccopies = []
-    for d in range(1, nx):
-        above, below = (2 if d == 1 else 0), (3 if d == nx - 1 else 1)
-        which = jnp.where(ix + d >= nx, below, above).astype(jnp.int32)
-        copy = pltpu.make_async_remote_copy(
-            cs.at[which], cr.at[d - 1], css.at[d - 1], crs.at[d - 1],
-            device_id={"gx": lax.rem(ix + d, nx)}, device_id_type=MESH)
-        copy.start()
-        ccopies.append(copy)
-
     arrive(h2x)
     halo_rows = [*range(3), *range(lx - 3, lx)]
     own_x = []
@@ -605,6 +604,16 @@
             for w, v in zip(weights, pieces):
                 total += float(w) * v
             inc[f, i] = total
+    for copy in ccopies:
+        copy.wait_recv()
+    sums = []
+    for at in (31, 31 + nx - 1):
+        total = xtab(at + 1) * cr[0]
+        for d in range(2, nx):
+            total += xtab(at + d) * cr[d - 1]
+        sums.append(total)
+    values = [side_by_side(sums[0], shifted(sums[1], lz)), side_by_side(shifted(sums[0], -lz), sums[1])]
+    vcopies, finish_sides = y_exchange(jnp.concatenate(values, 0), vs, vr, vss, vrs)
     outside = three(jnp.concatenate(finish(), 0), 0)
     for fs in pairs(5):
         far = dot(outside, jnp.concatenate([part("ey", f) for f in fs], 1), TN)
@@ -613,16 +622,7 @@
             for i in range(lx):
                 out[f, pl.ds(i, lz, stride=lx), :] = inc[f, i] + total[i]
 
-    for copy in ccopies:
-        copy.wait_recv()
-    sides = []
-    for at in (31, 31 + nx - 1):
-        total = xtab(at + 1) * cr[0]
-        for d in range(2, nx):
-            total += xtab(at + d) * cr[d - 1]
-        sides.append(jnp.concatenate([total, shifted(total, -lz)], 0))
-    lane = lax.broadcasted_iota(jnp.int32, (16, ly), 1)
-    outside = three(jnp.where(lane < lz, sides[0], jnp.where(lane < 2 * lz, shifted(sides[1], lz), 0.0)), 0)
+    outside = three(jnp.concatenate(finish_sides(), 0), 0)
     for copy in copies:
         copy.wait_recv()
     for fs in pairs(5):

time: 26.5 us -> 25.1 us (0.947)
  Pallas kernels: 24.9 us -> 23.5 us
    pallas_call x1, Pallas kernels: 24.9 us -> 23.5 us  [body(): pl.pallas_call(functools.partial(kernel, nx, ny, lx, lz, ly, coefficient,...]
where the time goes in v5:
time: 25.1 us; the launch traced here: 24.9 us
  Pallas kernels  23.5 us (94%)
  other arithmetic  1.4 us (6%)
    pallas_call x1, Pallas kernels, body(): pl.pallas_call(functools.partial(kernel, nx, ny, lx, lz, ly, coefficient,...  23.5 us
    add x1, other arithmetic, body(): return result.reshape(5, lz, lx, ly) + along[0] * low + along[1] * high  1.4 us

profile of v5, /device:TPU:1, one launch (start us, length us, event | category | flops | bytes accessed | tf_op | source)
XLA Modules:
  0.0 24.9 jit_solution(14841251117669817112)
XLA Ops:
  0.0 0.0 copy-start
  0.0 0.0 copy-start.1
  0.0 23.5 %shard_map.82 = (f32[5,512,128]{2,1,0:T(8,128)S(1)}, f32[5,16,128]{2,1,0:T(8,128)S(1)}, f32[5,16,128]{2,1,0:T(8,128)S(1)}) custom-call(f32[512,128]{1,0:T(8,128)} %bitcast.6, f32[3,512,128]{2,1,0:T(8,128)} %bitcast.5, f32[512,128]{1,0:T(8,128)} %bitcast.7, bf16[3056,128]{1,0:T(8,128)(2,1)} %constant.10.clone.tab_in, f32[368]{0:T(512)} %constant.11.clone.xt_in, ...), custom_call_target="tpu_custom_call" | custom-call | tf_op jit(solution)/shard_map/pallas_call | solution.py:661
  23.5 0.0 copy-done
  23.5 0.0 copy-done.1
  23.5 1.4 %multiply_add_fusion = f32[5,16,32,128]{3,2,1,0:T(8,128)} fusion(f32[5,16,32,128]{3,2,1,0:T(8,128)S(1)} %bitcast.4, f32[5,16,128]{2,1,0:T(8,128)S(1)} %get-tuple-element.10, f32[32]{0:T(128)S(1)} %copy-done, f32[5,16,128]{2,1,0:T(8,128)S(1)} %get-tuple-element.9, f32[32]{0:T(128)S(1)} %copy-done.1), kind=kLoop, calls=%fused_computation | loop fusion | flops 1310720 | bytes 2703616 | tf_op jit(solution)/shard_map/add | solution.py:716
Async XLA Ops:
  0.0 23.5 %copy-start = (f32[32]{0:T(128)S(1)}, f32[32]{0:T(128)}, u32[]{:S(2)}) copy-start(f32[32]{0:T(128)} %constant.14.clone) | copy-start | bytes 388
  0.0 23.5 %copy-start.1 = (f32[32]{0:T(128)S(1)}, f32[32]{0:T(128)}, u32[]{:S(2)}) copy-start(f32[32]{0:T(128)} %constant.13.clone) | copy-start | bytes 388

commit v6 on v5

--- a/solution.py
+++ b/solution.py
@@ -219,7 +219,7 @@
 def kernel(
     nx, ny, lx, lz, ly, coefficient, ipiv, xinv, alpha, beta, places,
     mass_in, mom_in, energy_in, tab_in, xt_in, yt_in, out, low_out, high_out,
-    mass, mom, energy, tab, xt, yt,
+    mass, energy, tab, xt, yt,
     xp, pt, ept, mt, gy, pre, fxp, fy, dz, inc, ysend, yhalo, ysend2, yhalo2,
     xs, xl, xr, ws, wr, vs, vr, cs, cr,
     hss, hrs, xss, xrs, wss, wrs, vss, vrs, css, crs, lsem, near_sem,
@@ -228,6 +228,29 @@
     rows = lx * lz
     scale = -2.0 * coefficient * STEP
 
+    def group(rows_in, k):
+        for i in rows_in:
+            pltpu.make_async_copy(mass_in.at[:, i], mass.at[i], lsem.at[k]).start()
+            pltpu.make_async_copy(mom_in.at[:, :, i], mt.at[:, i], lsem.at[k + 1]).start()
+            pltpu.make_async_copy(energy_in.at[:, i], energy.at[i], lsem.at[k + 2]).start()
+        whole = pl.ds(0, len(rows_in))
+
+        def wait():
+            for n, ref in enumerate((mass.at[whole], mt.at[:, whole], energy.at[whole])):
+                pltpu.make_async_copy(ref, ref, lsem.at[k + n]).wait()
+
+        return wait
+
+    edges = sorted({*range(3), *range(lx - 3, lx)})
+    edges_loaded = group(edges, 3)
+    inner_loaded = group(range(3, lx - 3), 6)
+    loads = [
+        pltpu.make_async_copy(a, b, lsem.at[k])
+        for k, (a, b) in enumerate(((tab_in, tab), (xt_in, xt), (yt_in, yt)))
+    ]
+    for load in loads:
+        load.start()
+
     barrier = pltpu.get_barrier_semaphore()
 
 
@@ -259,14 +282,6 @@
     for d in range(1, ny):
         pl.semaphore_signal(barrier, inc=1, device_id={"gy": lax.rem(iy + d, ny)}, device_id_type=MESH)
 
-    loads = [
-        pltpu.make_async_copy(a, b, lsem.at[k])
-        for k, (a, b) in enumerate((
-            (mass_in, mass), (mom_in, mom), (energy_in, energy), (tab_in, tab), (xt_in, xt), (yt_in, yt)))
-    ]
-    for load in loads:
-        load.start()
-
     def part(*name):
         low, high = places[name if len(name) > 1 else name[0]]
         return tab[low:high]
@@ -278,23 +293,19 @@
         return v.reshape(lx, lz, ly)
 
     def primitives(i, _=None):
-        at = pl.ds(i, lz, stride=lx)
-        rho, e = mass[at, :], energy[at, :]
-        m = [mom[k, at, :] for k in range(3)]
+        rho, e = mass[i], energy[i]
+        m = [mt[k, i] for k in range(3)]
         inv = 1.0 / rho
         u = [a * inv for a in m]
         p = 0.4 * (e - 0.5 * (m[0] * u[0] + m[1] * u[1] + m[2] * u[2]))
         for k in range(3):
             xp[k, i + 3] = u[k]
-            mt[k, i] = m[k]
         xp[3, i + 3] = p * inv
         pt[i] = p
         ept[i] = e + p
         return 0
 
-    for load in loads[:3]:
-        load.wait()
-    edges = sorted({*range(3), *range(lx - 3, lx)})
+    edges_loaded()
     for i in edges:
         primitives(i)
 
@@ -368,8 +379,9 @@
     pl.semaphore_wait(barrier, expected + (ny - 1))
     start(h1x)
     tell()
+    inner_loaded()
     lax.fori_loop(3, lx - 3, primitives, 0, unroll=2)
-    for load in loads[3:]:
+    for load in loads:
         load.wait()
     ysend[...] = packed(lambda f: xp[f, 3 : lx + 3], 4)
     h1y = y_halo(ysend, yhalo, 2)
@@ -435,10 +447,13 @@
     arrive(h1x)
     hear()
     tell()
-    for i in edges:
+    h2x = x_halo(fxp, 5, 4)
+    for i in range(3):
         fluxes(i, gradients(i))
-    h2x = x_halo(fxp, 5, 4)
-    start(h2x)
+    pl.when(ix > 0)(h2x[1].start)
+    for i in range(lx - 3, lx):
+        fluxes(i, gradients(i))
+    pl.when(ix < nx - 1)(h2x[0].start)
     ysend2[...] = packed(lambda f: fy[f], 5)
     h2y = y_halo(ysend2, yhalo2, 6)
     start(h2y)
@@ -597,8 +612,7 @@
     for f in range(5):
         pieces = [solved[lz * (8 * f + n) : lz * (8 * f + n + 1)] for n in range(8)]
         for i in range(lx):
-            at = pl.ds(i, lz, stride=lx)
-            state = mass[at, :] if f == 0 else (energy[at, :] if f == 4 else mt[f - 1, i])
+            state = mass[i] if f == 0 else (energy[i] if f == 4 else mt[f - 1, i])
             total = state + fy[f, i]
             weights = [alpha[i], beta[i], *(xinv[i, r] for r in halo_rows)]
             for w, v in zip(weights, pieces):
@@ -655,7 +669,7 @@
     block = (lx, lz, ly)
     dma = pltpu.SemaphoreType.DMA
     operands = (
-        mass.reshape(rows, ly), mom.reshape(3, rows, ly), energy.reshape(rows, ly),
+        mass, mom, energy,
         jnp.asarray(tab), jnp.asarray(xtab.reshape(-1)), jnp.asarray(ytab.reshape(-1)),
     )
     result, low, high = pl.pallas_call(
@@ -665,9 +679,8 @@
         in_specs=[hbm] * 6,
         out_specs=(vm, vm, vm),
         scratch_shapes=[
-            pltpu.VMEM((rows, ly), f32),
-            pltpu.VMEM((3, rows, ly), f32),
-            pltpu.VMEM((rows, ly), f32),
+            pltpu.VMEM(block, f32),
+            pltpu.VMEM(block, f32),
             pltpu.VMEM(tab.shape, jnp.bfloat16),
             pltpu.SMEM((xtab.size,), f32),
             pltpu.SMEM((ytab.size,), f32),
@@ -704,7 +717,7 @@
             dma((ny - 1,)),
             dma((nx - 1,)),
             dma((nx - 1,)),
-            dma((6,)),
+            dma((9,)),
             pltpu.SemaphoreType.REGULAR((max(1, (nx - 1).bit_length()),)),
         ],
         compiler_params=pltpu.CompilerParams(

time: 25.1 us -> 24.9 us (level)
  Pallas kernels: 23.5 us -> 23.1 us
    pallas_call x1, Pallas kernels: 23.5 us -> 23.1 us  [body(): pl.pallas_call(functools.partial(kernel, nx, ny, lx, lz, ly, coefficient,...]
where the time goes in v6:
time: 24.9 us; the launch traced here: 24.6 us
  Pallas kernels  23.1 us (93%)
  other arithmetic  1.4 us (6%)
    pallas_call x1, Pallas kernels, body(): pl.pallas_call(functools.partial(kernel, nx, ny, lx, lz, ly, coefficient,...  23.1 us
    add x1, other arithmetic, body(): return result.reshape(5, lz, lx, ly) + along[0] * low + along[1] * high  1.4 us

profile of v6, /device:TPU:1, one launch (start us, length us, event | category | flops | bytes accessed | tf_op | source)
XLA Modules:
  0.0 24.6 jit_solution(11948304306294421964)
XLA Ops:
  0.0 0.0 copy-start
  0.0 0.0 copy-start.1
  0.0 23.1 %shard_map.82 = (f32[5,512,128]{2,1,0:T(8,128)S(1)}, f32[5,16,128]{2,1,0:T(8,128)S(1)}, f32[5,16,128]{2,1,0:T(8,128)S(1)}) custom-call(f32[16,32,128]{2,1,0:T(8,128)} %mass_in.1, f32[3,16,32,128]{3,2,1,0:T(8,128)} %mom_in.1, f32[16,32,128]{2,1,0:T(8,128)} %energy_in.1, bf16[3056,128]{1,0:T(8,128)(2,1)} %constant.10.clone.tab_in, f32[368]{0:T(512)} %constant.11.clone.xt_in, ...), custom_call_target="tpu_custom_call" | custom-call | tf_op jit(solution)/shard_map/pallas_call | solution.py:675
  23.2 0.0 copy-done
  23.2 0.0 copy-done.1
  23.2 1.4 %multiply_add_fusion = f32[5,16,32,128]{3,2,1,0:T(8,128)} fusion(f32[5,16,32,128]{3,2,1,0:T(8,128)S(1)} %bitcast.1, f32[5,16,128]{2,1,0:T(8,128)S(1)} %get-tuple-element.10, f32[32]{0:T(128)S(1)} %copy-done, f32[5,16,128]{2,1,0:T(8,128)S(1)} %get-tuple-element.9, f32[32]{0:T(128)S(1)} %copy-done.1), kind=kLoop, calls=%fused_computation | loop fusion | flops 1310720 | bytes 2703616 | tf_op jit(solution)/shard_map/add | solution.py:729
Async XLA Ops:
  0.0 23.2 %copy-start = (f32[32]{0:T(128)S(1)}, f32[32]{0:T(128)}, u32[]{:S(2)}) copy-start(f32[32]{0:T(128)} %constant.14.clone) | copy-start | bytes 388
  0.0 23.2 %copy-start.1 = (f32[32]{0:T(128)S(1)}, f32[32]{0:T(128)}, u32[]{:S(2)}) copy-start(f32[32]{0:T(128)} %constant.13.clone) | copy-start | bytes 388

commit v7 on v6

--- a/solution.py
+++ b/solution.py
@@ -400,6 +400,15 @@
         return 0
 
     lax.fori_loop(3, lx - 3, ahead, 0, unroll=2)
+    for i in edges:
+        z = [around(xp[f, i + 3]) for f in range(4)]
+        for n, g in ((1, z[2]), (3, z[0]), (4, z[1]), (6, z[3])):
+            pre[n, i] = g
+
+    def at_edge(i):
+        x = [difference(lambda k: xp[f, i + 3 + k]) for f in range(4)]
+        return x[0], pre[1, i], x[1], x[2] + pre[3, i], pre[4, i], x[3], pre[6, i]
+
     arrive(h1y)
     hear()
     tell()
@@ -443,16 +452,16 @@
     def inner(i, _):
         return fluxes(i)
 
-    lax.fori_loop(3, lx - 3, inner, 0)
+    lax.fori_loop(3, lx - 3, inner, 0, unroll=2)
     arrive(h1x)
     hear()
     tell()
     h2x = x_halo(fxp, 5, 4)
     for i in range(3):
-        fluxes(i, gradients(i))
+        fluxes(i, at_edge(i))
     pl.when(ix > 0)(h2x[1].start)
     for i in range(lx - 3, lx):
-        fluxes(i, gradients(i))
+        fluxes(i, at_edge(i))
     pl.when(ix < nx - 1)(h2x[0].start)
     ysend2[...] = packed(lambda f: fy[f], 5)
     h2y = y_halo(ysend2, yhalo2, 6)

time: 24.9 us -> 24.7 us (level)
  no operation moved by 1% of the time
where the time goes in v7:
time: 24.7 us; the launch traced here: 24.5 us
  Pallas kernels  23.1 us (94%)
  other arithmetic  1.4 us (6%)
    pallas_call x1, Pallas kernels, body(): pl.pallas_call(functools.partial(kernel, nx, ny, lx, lz, ly, coefficient,...  23.1 us
    add x1, other arithmetic, body(): return result.reshape(5, lz, lx, ly) + along[0] * low + along[1] * high  1.4 us

profile of v7, /device:TPU:1, one launch (start us, length us, event | category | flops | bytes accessed | tf_op | source)
XLA Modules:
  0.0 24.5 jit_solution(3599197219681015067)
XLA Ops:
  0.0 0.0 copy-start
  0.0 0.0 copy-start.1
  0.0 23.1 %shard_map.82 = (f32[5,512,128]{2,1,0:T(8,128)S(1)}, f32[5,16,128]{2,1,0:T(8,128)S(1)}, f32[5,16,128]{2,1,0:T(8,128)S(1)}) custom-call(f32[16,32,128]{2,1,0:T(8,128)} %mass_in.1, f32[3,16,32,128]{3,2,1,0:T(8,128)} %mom_in.1, f32[16,32,128]{2,1,0:T(8,128)} %energy_in.1, bf16[3056,128]{1,0:T(8,128)(2,1)} %constant.10.clone.tab_in, f32[368]{0:T(512)} %constant.11.clone.xt_in, ...), custom_call_target="tpu_custom_call" | custom-call | tf_op jit(solution)/shard_map/pallas_call | solution.py:684
  23.1 0.0 copy-done
  23.1 0.0 copy-done.1
  23.1 1.4 %multiply_add_fusion = f32[5,16,32,128]{3,2,1,0:T(8,128)} fusion(f32[5,16,32,128]{3,2,1,0:T(8,128)S(1)} %bitcast.1, f32[5,16,128]{2,1,0:T(8,128)S(1)} %get-tuple-element.10, f32[32]{0:T(128)S(1)} %copy-done, f32[5,16,128]{2,1,0:T(8,128)S(1)} %get-tuple-element.9, f32[32]{0:T(128)S(1)} %copy-done.1), kind=kLoop, calls=%fused_computation | loop fusion | flops 1310720 | bytes 2703616 | tf_op jit(solution)/shard_map/add | solution.py:738
Async XLA Ops:
  0.0 23.1 %copy-start = (f32[32]{0:T(128)S(1)}, f32[32]{0:T(128)}, u32[]{:S(2)}) copy-start(f32[32]{0:T(128)} %constant.14.clone) | copy-start | bytes 388
  0.0 23.1 %copy-start.1 = (f32[32]{0:T(128)S(1)}, f32[32]{0:T(128)}, u32[]{:S(2)}) copy-start(f32[32]{0:T(128)} %constant.13.clone) | copy-start | bytes 388

commit v8 on v7

--- a/solution.py
+++ b/solution.py
@@ -558,7 +558,7 @@
     for w in range(4):
         cs[w] = side_by_side(shifted(values[0:8], -lz * w), shifted(values[8:16], lz - lz * w))
     ccopies = []
-    for d in range(1, nx):
+    for d in sorted(range(1, nx), key=lambda d: -min(d, nx - d)):
         above, below = (2 if d == 1 else 0), (3 if d == nx - 1 else 1)
         which = jnp.where(ix + d >= nx, below, above).astype(jnp.int32)
         copy = pltpu.make_async_remote_copy(
@@ -567,7 +567,7 @@
         copy.start()
         ccopies.append(copy)
     copies = []
-    for d in range(1, nx):
+    for d in sorted(range(1, nx), key=lambda d: -min(d, nx - d)):
         above, below = (2 if d == 1 else 0), (3 if d == nx - 1 else 1)
         which = jnp.where(ix + d >= nx, below, above).astype(jnp.int32)
         copy = pltpu.make_async_remote_copy(

time: 24.7 us -> 25.1 us (1.016)
  Pallas kernels: 23.1 us -> 23.5 us
    pallas_call x1, Pallas kernels: 23.1 us -> 23.5 us  [body(): pl.pallas_call(functools.partial(kernel, nx, ny, lx, lz, ly, coefficient,...]
where the time goes in v8:
time: 25.1 us; the launch traced here: 24.9 us
  Pallas kernels  23.5 us (94%)
  other arithmetic  1.4 us (6%)
    pallas_call x1, Pallas kernels, body(): pl.pallas_call(functools.partial(kernel, nx, ny, lx, lz, ly, coefficient,...  23.5 us
    add x1, other arithmetic, body(): return result.reshape(5, lz, lx, ly) + along[0] * low + along[1] * high  1.4 us

profile of v8, /device:TPU:1, one launch (start us, length us, event | category | flops | bytes accessed | tf_op | source)
XLA Modules:
  0.0 24.9 jit_solution(7207010736485240184)
XLA Ops:
  0.0 0.0 copy-start
  0.0 0.0 copy-start.1
  0.0 23.5 %shard_map.82 = (f32[5,512,128]{2,1,0:T(8,128)S(1)}, f32[5,16,128]{2,1,0:T(8,128)S(1)}, f32[5,16,128]{2,1,0:T(8,128)S(1)}) custom-call(f32[16,32,128]{2,1,0:T(8,128)} %mass_in.1, f32[3,16,32,128]{3,2,1,0:T(8,128)} %mom_in.1, f32[16,32,128]{2,1,0:T(8,128)} %energy_in.1, bf16[3056,128]{1,0:T(8,128)(2,1)} %constant.10.clone.tab_in, f32[368]{0:T(512)} %constant.11.clone.xt_in, ...), custom_call_target="tpu_custom_call" | custom-call | tf_op jit(solution)/shard_map/pallas_call | solution.py:684
  23.5 0.0 copy-done
  23.5 0.0 copy-done.1
  23.5 1.4 %multiply_add_fusion = f32[5,16,32,128]{3,2,1,0:T(8,128)} fusion(f32[5,16,32,128]{3,2,1,0:T(8,128)S(1)} %bitcast.1, f32[5,16,128]{2,1,0:T(8,128)S(1)} %get-tuple-element.10, f32[32]{0:T(128)S(1)} %copy-done, f32[5,16,128]{2,1,0:T(8,128)S(1)} %get-tuple-element.9, f32[32]{0:T(128)S(1)} %copy-done.1), kind=kLoop, calls=%fused_computation | loop fusion | flops 1310720 | bytes 2703616 | tf_op jit(solution)/shard_map/add | solution.py:738
Async XLA Ops:
  0.0 23.5 %copy-start = (f32[32]{0:T(128)S(1)}, f32[32]{0:T(128)}, u32[]{:S(2)}) copy-start(f32[32]{0:T(128)} %constant.14.clone) | copy-start | bytes 388
  0.0 23.5 %copy-start.1 = (f32[32]{0:T(128)S(1)}, f32[32]{0:T(128)}, u32[]{:S(2)}) copy-start(f32[32]{0:T(128)} %constant.13.clone) | copy-start | bytes 388
